TPU v7x, 32 devices: a whole 2x2x4 slice. The times are simulated.
32 devices in a mesh: fsdp: 4 (over z), ctx: 2 (over core), tp: 4 (over y, x).
Axes of the slice: x: 2, y: 2, z: 4, core: 2. Of those that a mesh axis runs over, the one named last changes fastest.
Arguments:
- tokens: bfloat16 [16, 1024, 768], P('fsdp', 'ctx'), may hold values from -6 to 6
- lengths: int32 [16], P('fsdp'), may hold values from 256 to 1024, as said below
- qkv_weight: bfloat16 [3, 768, 768], P(None, 'fsdp', 'tp'), may hold values from -0.21875 to 0.21875
- qv_bias: float32 [2, 768], P(None, 'tp'), may hold values from -3 to 3
- out_weight: bfloat16 [768, 768], P('tp', 'fsdp'), may hold values from -1.75 to 1.75
- out_bias: float32 [768], replicated, may hold values from -3 to 3
- ffn_in: bfloat16 [768, 3072], P('fsdp', 'tp'), may hold values from -0.21875 to 0.21875
- ffn_in_bias: float32 [3072], P('tp'), may hold values from -3 to 3
- ffn_out: bfloat16 [3072, 768], P('tp', 'fsdp'), may hold values from -0.109375 to 0.109375
- ffn_out_bias: float32 [768], replicated, may hold values from -3 to 3
- norm_gains: float32 [2, 768], replicated, may hold values from 0.1 to 1.9
- norm_shifts: float32 [2, 768], replicated, may hold values from -3 to 3
- cotangent: bfloat16 [16, 1024, 768], P('fsdp', 'ctx'), may hold values from -6 to 6
Outputs:
- layer_output: bfloat16 [16, 1024, 768], P('fsdp', 'ctx')
- grad_tokens: float32 [16, 1024, 768], P('fsdp', 'ctx')
- grad_qkv_weight: float32 [3, 768, 768], P(None, 'fsdp', 'tp')
- grad_qv_bias: float32 [2, 768], P(None, 'tp')
- grad_out_weight: float32 [768, 768], P('tp', 'fsdp')
- grad_out_bias: float32 [768], replicated
- grad_ffn_in: float32 [768, 3072], P('fsdp', 'tp')
- grad_ffn_in_bias: float32 [3072], P('tp')
- grad_ffn_out: float32 [3072, 768], P('tp', 'fsdp')
- grad_ffn_out_bias: float32 [768], replicated
- grad_norm_gains: float32 [2, 768], replicated
- grad_norm_shifts: float32 [2, 768], replicated
Inputs may be any that keep to these rules, and one draw needn't show every extreme that they name: `lengths`: positions at or past a sequence's length are padding. Some sequence has exactly 1024 valid tokens and another exactly 256.
All inputs are finite; a program needn't handle non-finite values.
Results may differ from a plain program's by a relative error of at most 0.02.
Values may be sent and summed in bfloat16 or wider, within the bound.
No kernel may reach another device: no remote copies, remote signals or barrier semaphores. Data moves between devices by JAX's collectives and lax.ppermute only.
A program may use at most 192 MiB of HBM per device.

v0:
```python
import jax
import jax.numpy as jnp
from jax import lax
from jax.sharding import PartitionSpec as P

D = 768
HD = 64
FF = 3072
MICRO = 2


epsilon = 1e-05
masked_score = -1000000000.0


def layer_norm(residual, gain_row, shift_row):
    center = jnp.mean(residual, axis=-1, keepdims=True)
    centred = residual - center
    spread = jnp.mean(centred * centred, axis=-1, keepdims=True)
    return centred * lax.rsqrt(spread + epsilon) * gain_row + shift_row


def gelu_exact(hidden):
    return jax.nn.gelu(hidden, approximate=False)


def fetch_weights(qkv_weight, out_weight, ffn_in, ffn_out):
    return (
        lax.all_gather(qkv_weight, "fsdp", axis=1, tiled=True),
        lax.all_gather(out_weight, "fsdp", axis=1, tiled=True),
        lax.all_gather(ffn_in, "fsdp", axis=0, tiled=True),
        lax.all_gather(ffn_out, "fsdp", axis=1, tiled=True),
    )


def owned_grads(grad_qkv, grad_out, grad_in, grad_down):
    return (
        lax.psum_scatter(
            grad_qkv.astype(jnp.bfloat16), "fsdp", scatter_dimension=1, tiled=True
        ).astype(jnp.float32),
        lax.psum_scatter(
            grad_out.astype(jnp.bfloat16), "fsdp", scatter_dimension=1, tiled=True
        ).astype(jnp.float32),
        lax.psum_scatter(
            grad_in.astype(jnp.bfloat16), "fsdp", scatter_dimension=0, tiled=True
        ).astype(jnp.float32),
        lax.psum_scatter(
            grad_down.astype(jnp.bfloat16), "fsdp", scatter_dimension=1, tiled=True
        ).astype(jnp.float32),
    )


def score_block(queries, keys_all, length):
    dot_scores = jnp.einsum("qhd,khd->hqk", queries, keys_all, preferred_element_type=jnp.float32)
    key_valid = jnp.arange(keys_all.shape[0], dtype=jnp.int32) < length
    return jnp.where(key_valid[None, None, :], dot_scores * 0.125, masked_score)


def attend(queries, keys_all, values_all, length):
    scores = score_block(queries, keys_all, length)
    row_max = jnp.max(scores, axis=-1, keepdims=True)
    exponent = jnp.exp(scores - row_max)
    row_sum = jnp.sum(exponent, axis=-1, keepdims=True)
    weights_low = (exponent / row_sum).astype(jnp.bfloat16)
    context = jnp.einsum(
        "hqk,khd->qhd", weights_low, values_all, preferred_element_type=jnp.float32
    )
    return (context.astype(jnp.bfloat16), row_max + jnp.log(row_sum))


def attend_back(queries, keys_all, values_all, length, log_total, grad_context):
    scores = score_block(queries, keys_all, length)
    probability = jnp.exp(scores - log_total)
    grad_values = jnp.einsum(
        "hqk,qhd->khd",
        probability.astype(jnp.bfloat16),
        grad_context,
        preferred_element_type=jnp.float32,
    )
    grad_probs = jnp.einsum(
        "qhd,khd->hqk", grad_context, values_all, preferred_element_type=jnp.float32
    )
    inner_sum = jnp.sum(probability * grad_probs, axis=-1, keepdims=True)
    grad_scores = (probability * (grad_probs - inner_sum) * 0.125).astype(jnp.bfloat16)
    grad_queries = jnp.einsum(
        "hqk,khd->qhd", grad_scores, keys_all, preferred_element_type=jnp.float32
    )
    grad_keys = jnp.einsum("hqk,qhd->khd", grad_scores, queries, preferred_element_type=jnp.float32)
    return (grad_queries, grad_keys, grad_values)


def add_trees(first_tree, second_tree):
    if first_tree is None:
        return second_tree
    return jax.tree.map(jnp.add, first_tree, second_tree)


def per_device(
    tokens,
    lengths,
    qkv_weight,
    qv_bias,
    out_weight,
    out_bias,
    ffn_in,
    ffn_in_bias,
    ffn_out,
    ffn_out_bias,
    norm_gains,
    norm_shifts,
    cotangent,
):
    seq_micro = tokens.shape[0] // MICRO
    local_len = tokens.shape[1]
    model_width = tokens.shape[2]
    local_feat = qkv_weight.shape[2]
    local_units = ffn_in.shape[1]
    heads_local = local_feat // HD
    row_count = seq_micro * local_len
    tp_rank = lax.axis_index("tp")
    share = row_count // lax.axis_size("tp")
    row_start = tp_rank * share
    row_ids = jnp.arange(row_count, dtype=jnp.int32)
    share_mask = ((row_ids >= row_start) & (row_ids < row_start + share)).astype(jnp.float32)[
        :, None
    ]
    positions = lax.axis_index("ctx") * local_len + jnp.arange(local_len, dtype=jnp.int32)
    zero_bias = jnp.zeros_like(qv_bias[0])
    bias_stack = jnp.stack((qv_bias[0], zero_bias, qv_bias[1]))[:, None, :]
    owned_total = None
    small_total = None
    outputs_list = []
    grad_rows_list = []
    for micro_index in range(MICRO):
        fetched = fetch_weights(qkv_weight, out_weight, ffn_in, ffn_out)
        full_qkv, full_out, full_in, full_down = fetched
        lower = micro_index * seq_micro
        upper = lower + seq_micro
        flat_rows = tokens[lower:upper].reshape(row_count, model_width)
        lengths_micro = lengths[lower:upper]
        projected = jnp.einsum(
            "rd,tde->tre", flat_rows, full_qkv, preferred_element_type=jnp.float32
        )
        qkv_low = (projected + bias_stack).astype(jnp.bfloat16)
        key_value = qkv_low[1:3].reshape(2, seq_micro, local_len, local_feat)
        key_value_all = lax.all_gather(key_value, "ctx", axis=2, tiled=True)
        full_len = key_value_all.shape[2]
        query_heads = qkv_low[0].reshape(seq_micro, local_len, heads_local, HD)
        key_heads = key_value_all[0].reshape(seq_micro, full_len, heads_local, HD)
        value_heads = key_value_all[1].reshape(seq_micro, full_len, heads_local, HD)
        context_list = []
        totals_list = []
        for sequence in range(seq_micro):
            context_seq, log_total = attend(
                query_heads[sequence],
                key_heads[sequence],
                value_heads[sequence],
                lengths_micro[sequence],
            )
            context_list.append(context_seq)
            totals_list.append(log_total)
        context = jnp.stack(context_list).reshape(row_count, local_feat)
        inputs_float = flat_rows.astype(jnp.float32)
        row_valid = (
            (positions[None, :] < lengths_micro[:, None]).astype(jnp.float32).reshape(row_count, 1)
        )
        grad_output = (
            cotangent[lower:upper].reshape(row_count, model_width).astype(jnp.float32) * row_valid
        )
        attn_part = jnp.dot(context, full_out, preferred_element_type=jnp.float32)
        attended = lax.psum(attn_part.astype(jnp.bfloat16), "tp").astype(jnp.float32) + out_bias
        residual_one = inputs_float + attended
        normed, first_pull = jax.vjp(layer_norm, residual_one, norm_gains[0], norm_shifts[0])
        normed_low = normed.astype(jnp.bfloat16)
        hidden = jnp.dot(normed_low, full_in, preferred_element_type=jnp.float32) + ffn_in_bias
        activated, gelu_pull = jax.vjp(gelu_exact, hidden)
        activated_low = activated.astype(jnp.bfloat16)
        branch_part = jnp.dot(activated_low, full_down, preferred_element_type=jnp.float32)
        branch = lax.psum(branch_part.astype(jnp.bfloat16), "tp").astype(jnp.float32) + ffn_out_bias
        output, second_pull = jax.vjp(layer_norm, normed + branch, norm_gains[1], norm_shifts[1])
        grad_second = second_pull(grad_output)[0]
        _, grad_gain_two, grad_shift_two = second_pull(grad_output * share_mask)
        grad_branch = grad_second.astype(jnp.bfloat16)
        grad_down_bias = jnp.sum(
            lax.dynamic_slice_in_dim(grad_branch, row_start, share, 0).astype(jnp.float32), axis=0
        )
        grad_down = jnp.einsum(
            "rf,rd->fd", activated_low, grad_branch, preferred_element_type=jnp.float32
        )
        grad_activated = jnp.einsum(
            "rd,fd->rf", grad_branch, full_down, preferred_element_type=jnp.float32
        )
        grad_hidden = gelu_pull(grad_activated)[0].astype(jnp.bfloat16)
        grad_in_bias = jnp.sum(grad_hidden.astype(jnp.float32), axis=0)
        grad_in = jnp.einsum(
            "rd,rf->df", normed_low, grad_hidden, preferred_element_type=jnp.float32
        )
        normed_part = jnp.einsum(
            "rf,df->rd", grad_hidden, full_in, preferred_element_type=jnp.float32
        )
        grad_normed = (
            lax.psum(normed_part.astype(jnp.bfloat16), "tp").astype(jnp.float32) + grad_second
        )
        grad_first = first_pull(grad_normed)[0]
        _, grad_gain_one, grad_shift_one = first_pull(grad_normed * share_mask)
        grad_attended = grad_first.astype(jnp.bfloat16)
        grad_out_bias = jnp.sum(
            lax.dynamic_slice_in_dim(grad_attended, row_start, share, 0).astype(jnp.float32), axis=0
        )
        grad_out = jnp.einsum(
            "re,rd->ed", context, grad_attended, preferred_element_type=jnp.float32
        )
        grad_context = jnp.einsum(
            "rd,ed->re", grad_attended, full_out, preferred_element_type=jnp.float32
        )
        grad_context = grad_context.astype(jnp.bfloat16).reshape(
            seq_micro, local_len, heads_local, HD
        )
        query_grads = []
        key_grads = []
        value_grads = []
        for sequence in range(seq_micro):
            grad_q_seq, grad_k_seq, grad_v_seq = attend_back(
                query_heads[sequence],
                key_heads[sequence],
                value_heads[sequence],
                lengths_micro[sequence],
                totals_list[sequence],
                grad_context[sequence],
            )
            query_grads.append(grad_q_seq)
            key_grads.append(grad_k_seq)
            value_grads.append(grad_v_seq)
        grad_key_value = jnp.stack((jnp.stack(key_grads), jnp.stack(value_grads))).reshape(
            2, seq_micro, full_len, local_feat
        )
        key_value_grad = lax.psum_scatter(
            grad_key_value.astype(jnp.bfloat16), "ctx", scatter_dimension=2, tiled=True
        ).astype(jnp.float32)
        grad_query_low = (
            jnp.stack(query_grads).reshape(1, row_count, local_feat).astype(jnp.bfloat16)
        )
        grad_kv_low = key_value_grad.reshape(2, row_count, local_feat).astype(jnp.bfloat16)
        grad_qkv_low = jnp.concatenate((grad_query_low, grad_kv_low), axis=0)
        qkv_sums = jnp.sum(grad_qkv_low.astype(jnp.float32), axis=1)
        grad_bias_qv = jnp.stack((qkv_sums[0], qkv_sums[2]))
        grad_qkv = jnp.einsum(
            "rd,tre->tde", flat_rows, grad_qkv_low, preferred_element_type=jnp.float32
        )
        input_part = jnp.einsum(
            "tre,tde->rd", grad_qkv_low, full_qkv, preferred_element_type=jnp.float32
        )
        grad_all = lax.psum(input_part.astype(jnp.bfloat16), "tp").astype(jnp.float32) + grad_first
        output_rows = output.astype(jnp.bfloat16)
        outputs_list.append(output_rows.reshape(seq_micro, local_len, model_width))
        grad_rows_list.append(grad_all.reshape(seq_micro, local_len, model_width))
        qv_wide = lax.dynamic_update_slice_in_dim(
            jnp.zeros((2, D), jnp.float32), grad_bias_qv, tp_rank * local_feat, 1
        )
        in_wide = lax.dynamic_update_slice_in_dim(
            jnp.zeros((FF,), jnp.float32), grad_in_bias, tp_rank * local_units, 0
        )
        gains_pair = jnp.stack((grad_gain_one, grad_gain_two))
        shifts_pair = jnp.stack((grad_shift_one, grad_shift_two))
        micro_small = (qv_wide, grad_out_bias, in_wide, grad_down_bias, gains_pair, shifts_pair)
        small_total = add_trees(small_total, micro_small)
        owned_micro = owned_grads(grad_qkv, grad_out, grad_in, grad_down)
        owned_total = add_trees(owned_total, owned_micro)
    owned_sum = (
        lax.psum(owned_total[0].astype(jnp.bfloat16), "ctx").astype(jnp.float32),
        lax.psum(owned_total[1].astype(jnp.bfloat16), "ctx").astype(jnp.float32),
        lax.psum(owned_total[2].astype(jnp.bfloat16), "ctx").astype(jnp.float32),
        lax.psum(owned_total[3].astype(jnp.bfloat16), "ctx").astype(jnp.float32),
    )
    small_sum = lax.psum(
        (
            small_total[0],
            small_total[1],
            small_total[2],
            small_total[3],
            small_total[4],
            small_total[5],
        ),
        ("fsdp", "ctx", "tp"),
    )
    qv_mine = lax.dynamic_slice_in_dim(small_sum[0], tp_rank * local_feat, local_feat, 1)
    in_mine = lax.dynamic_slice_in_dim(small_sum[2], tp_rank * local_units, local_units, 0)
    return (
        jnp.concatenate(outputs_list, axis=0),
        jnp.concatenate(grad_rows_list, axis=0),
        owned_sum[0],
        qv_mine,
        owned_sum[1],
        small_sum[1],
        owned_sum[2],
        in_mine,
        owned_sum[3],
        small_sum[3],
        small_sum[4],
        small_sum[5],
    )


def solution(mesh):
    placed = (
        P("fsdp", "ctx", None),
        P("fsdp"),
        P(None, "fsdp", "tp"),
        P(None, "tp"),
        P("tp", "fsdp"),
        P(),
        P("fsdp", "tp"),
        P("tp"),
        P("tp", "fsdp"),
        P(),
        P(),
        P(),
        P("fsdp", "ctx", None),
    )
    return jax.shard_map(
        per_device,
        mesh=mesh,
        in_specs=placed,
        out_specs=(
            P("fsdp", "ctx", None),
            P("fsdp", "ctx", None),
            P(None, "fsdp", "tp"),
            P(None, "tp"),
            P("tp", "fsdp"),
            P(),
            P("fsdp", "tp"),
            P("tp"),
            P("tp", "fsdp"),
            P(),
            P(),
            P(),
        ),
        check_vma=False,
    )
```

profile of v0, /device:TPU:0, one launch (start us, length us, event | category | flops | bytes accessed | tf_op | source)
XLA Modules:
  0.0 925.4 jit_solution(9085310478080713553)
XLA Ops:
  10.0 31.5 %all_gather.22 = bf16[3,768,192]{2,0,1:T(4,128)(2,1)S(1)} all-gather(bf16[3,192,192]{2,0,1:T(4,128)(2,1)S(1)} %copy.43), channel_id=1, replica_groups=mesh['fsdp'=4,'ctx'=2,'tp'=4] {'fsdp'}, dimensions={1}, use_global_device_ids=true | all-gather | bytes 1105920 | tf_op jit(solution)/shard_map/all_gather | solution.py:29
  41.5 2.7 fusion.212
  47.2 2.9 fusion.109
  60.7 14.7 %all_gather.24 = bf16[192,768]{0,1:T(8,128)(2,1)S(1)} all-gather(bf16[192,192]{0,1:T(8,128)(2,1)} %copy.47), channel_id=1, replica_groups=mesh['fsdp'=4,'ctx'=2,'tp'=4] {'fsdp'}, dimensions={1}, use_global_device_ids=true | all-gather | bytes 368640 | tf_op jit(solution)/shard_map/all_gather | solution.py:30
  80.6 2.1 fusion.165
  109.0 86.1 %all-reduce.18.cloned.1.call-done = (bf16[1024,768]{1,0:T(8,128)(2,1)}, bf16[1024,768]{1,0:T(8,128)(2,1)}) async-done(((bf16[1024,768]{1,0:T(8,128)(2,1)}, bf16[1024,768]{1,0:T(8,128)(2,1)}), (bf16[1024,768]{1,0:T(8,128)(2,1)}, bf16[1024,768]{1,0:T(8,128)(2,1)})) %all-reduce.18.cloned.1.call-update) | async-done | bytes 3145744 | tf_op jit(solution)/shard_map/psum | solution.py:171
  195.2 3.1 fusion.103
  198.3 4.3 multiply_reduce_fusion.15
  204.5 2.9 fusion.200
  209.1 16.9 %multiply_convert_fusion.4 = (bf16[1024,768]{1,0:T(8,128)(2,1)}, f32[1024,768]{1,0:T(8,128)}, bf16[1024,768]{1,0:T(8,128)(2,1)}, f32[1024,768]{1,0:T(8,128)}, f32[1024,768]{1,0:T(8,128)}) fusion(f32[768]{0:T(1024)S(1)} %copy-done.113, f32[1024,768]{1,0:T(8,128)S(1)} %fusion.200, bf16[768,768]{1,0:T(8,128)(2,1)S(1)} %copy-done.109, ...), kind=kOutput, calls=%fused_computation.99 | convolution fusion | flops 1314914304 | bytes 20067328 | tf_op jit(solution)/shard_map/dot_general | solution.py:175
  226.0 4.5 convolution_convert_fusion.2
  230.5 2.7 convolution_convert_fusion.4
  236.5 83.8 %all-reduce.16.cloned.1.call-done = (bf16[1024,768]{1,0:T(8,128)(2,1)}, bf16[1024,768]{1,0:T(8,128)(2,1)}) async-done(((bf16[1024,768]{1,0:T(8,128)(2,1)}, bf16[1024,768]{1,0:T(8,128)(2,1)}), (bf16[1024,768]{1,0:T(8,128)(2,1)}, bf16[1024,768]{1,0:T(8,128)(2,1)})) %all-reduce.16.cloned.1.call-update) | async-done | bytes 3145744 | tf_op jit(solution)/shard_map/psum | solution.py:179
  320.3 4.1 fusion.206
  326.3 3.8 multiply_reduce_fusion.8
  330.2 4.6 fusion.205
  343.0 5.0 convert_reduce_fusion
  348.0 2.6 convolution_convert_fusion
  350.6 2.6 convolution_convert_fusion.1
  358.5 81.8 %all-reduce.14.cloned.1.call-done = (bf16[1024,768]{1,0:T(8,128)(2,1)}, bf16[1024,768]{1,0:T(8,128)(2,1)}) async-done(((bf16[1024,768]{1,0:T(8,128)(2,1)}, bf16[1024,768]{1,0:T(8,128)(2,1)}), (bf16[1024,768]{1,0:T(8,128)(2,1)}, bf16[1024,768]{1,0:T(8,128)(2,1)})) %all-reduce.14.cloned.1.call-update) | async-done | bytes 3145744 | tf_op jit(solution)/shard_map/psum | solution.py:202
  440.4 7.8 multiply_reduce_fusion.9
  448.6 4.9 fusion.202
  455.9 4.2 fusion.230
  462.1 3.6 fusion.229
  465.8 1.9 fusion.112
  467.7 18.0 %fusion.133 = bf16[3,64,1024]{2,1,0:T(8,128)(2,1)} fusion(bf16[512,3,64]{0,2,1:T(8,128)(2,1)} %bitcast.305, f32[3,512,1024]{2,1,0:T(8,128)} %fusion.229, f32[3,512,1024]{2,1,0:T(8,128)} %copy-done.3, f32[3,512]{1,0:T(4,128)} %log_add_fusion.3), kind=kOutput, calls=%fused_computation.193 | convolution fusion | flops 212535808 | bytes 13178880 | tf_op jit(solution)/shard_map/hqk,qhd->khd/dot_general | solution.py:88
  485.7 18.4 %fusion.130 = bf16[3,64,1024]{2,1,0:T(8,128)(2,1)} fusion(bf16[512,3,64]{0,2,1:T(8,128)(2,1)} %bitcast.303, f32[3,512,1024]{2,1,0:T(8,128)} %fusion.230, f32[3,512,1024]{2,1,0:T(8,128)} %copy-done.2, f32[3,512]{1,0:T(4,128)} %log_add_fusion.2), kind=kOutput, calls=%fused_computation.192 | convolution fusion | flops 212535808 | bytes 13178880 | tf_op jit(solution)/shard_map/hqk,qhd->khd/dot_general | solution.py:88
  504.1 2.6 maximum_maximum_fusion
  507.5 2.2 add_convert_fusion.4
  511.6 3.8 fusion.231
  515.4 18.3 %fusion.127 = bf16[3,64,1024]{2,1,0:T(8,128)(2,1)} fusion(bf16[512,3,64]{0,2,1:T(8,128)(2,1)} %bitcast.301, f32[3,512,1024]{2,1,0:T(8,128)} %fusion.231, f32[3,512,1024]{2,1,0:T(8,128)} %copy-done.1, f32[3,512]{1,0:T(4,128)} %log_add_fusion.1), kind=kOutput, calls=%fused_computation.191 | convolution fusion | flops 212535808 | bytes 13178880 | tf_op jit(solution)/shard_map/hqk,qhd->khd/dot_general | solution.py:88
  533.7 4.7 fusion.232
  538.4 18.0 %fusion.124 = bf16[3,64,1024]{2,1,0:T(8,128)(2,1)} fusion(bf16[512,3,64]{0,2,1:T(8,128)(2,1)} %bitcast.299, f32[3,512,1024]{2,1,0:T(8,128)} %fusion.232, f32[3,512,1024]{2,1,0:T(8,128)} %copy-done, f32[3,512]{1,0:T(4,128)} %log_add_fusion), kind=kOutput, calls=%fused_computation.190 | convolution fusion | flops 212535808 | bytes 13178880 | tf_op jit(solution)/shard_map/hqk,qhd->khd/dot_general | solution.py:88
  556.4 3.9 fusion.121
  560.3 4.2 fusion.118
  566.0 4.3 convolution_convert_fusion.6
  570.4 4.7 convolution_convert_fusion.7
  575.1 5.0 convolution_convert_fusion.8
  580.2 4.1 convolution_convert_fusion.9
  584.4 2.0 convolution_convert_fusion.14
  588.9 15.9 %fusion.152 = bf16[1,512,3,64]{1,3,2,0:T(8,128)(2,1)S(1)} fusion(bf16[1024,3,64]{0,2,1:T(8,128)(2,1)S(1)} %bitcast.280, f32[3,512,1024]{2,1,0:T(8,128)} %fusion.229, f32[3,512,1024]{2,1,0:T(8,128)} %copy-done.3, f32[3,512]{1,0:T(4,128)} %log_add_fusion.3), kind=kOutput, calls=%fused_computation.204 | convolution fusion | flops 212437504 | bytes 13178880 | tf_op jit(solution)/shard_map/hqk,khd->qhd/dot_general | solution.py:85
  604.8 15.9 %fusion.155 = bf16[1,512,3,64]{1,3,2,0:T(8,128)(2,1)S(1)} fusion(bf16[1024,3,64]{0,2,1:T(8,128)(2,1)S(1)} %bitcast.278, f32[3,512,1024]{2,1,0:T(8,128)} %fusion.230, f32[3,512,1024]{2,1,0:T(8,128)} %copy-done.2, f32[3,512]{1,0:T(4,128)} %log_add_fusion.2), kind=kOutput, calls=%fused_computation.205 | convolution fusion | flops 212437504 | bytes 13178880 | tf_op jit(solution)/shard_map/hqk,khd->qhd/dot_general | solution.py:85
  623.3 2.0 fusion.110
  625.3 2.6 copy.58
  627.9 2.2 reshape.458
  630.2 16.2 %fusion.158 = bf16[1,512,3,64]{1,3,2,0:T(8,128)(2,1)S(1)} fusion(bf16[1024,3,64]{0,2,1:T(8,128)(2,1)S(1)} %bitcast.276, f32[3,512,1024]{2,1,0:T(8,128)} %fusion.231, f32[3,512,1024]{2,1,0:T(8,128)} %copy-done.1, f32[3,512]{1,0:T(4,128)} %log_add_fusion.1), kind=kOutput, calls=%fused_computation.206 | convolution fusion | flops 212437504 | bytes 13178880 | tf_op jit(solution)/shard_map/hqk,khd->qhd/dot_general | solution.py:85
  646.5 15.6 %fusion.161 = bf16[1,512,3,64]{1,3,2,0:T(8,128)(2,1)S(1)} fusion(bf16[1024,3,64]{0,2,1:T(8,128)(2,1)S(1)} %bitcast.274, f32[3,512,1024]{2,1,0:T(8,128)} %fusion.232, f32[3,512,1024]{2,1,0:T(8,128)} %copy-done, f32[3,512]{1,0:T(4,128)} %log_add_fusion), kind=kOutput, calls=%fused_computation.207 | convolution fusion | flops 212437504 | bytes 13178880 | tf_op jit(solution)/shard_map/hqk,khd->qhd/dot_general | solution.py:85
  665.8 3.3 fusion.111
  669.1 2.5 copy.60
  671.7 2.3 reshape.460
  675.9 23.5 %reduce-scatter.23.cloned.1.call-done = bf16[192,768]{1,0:T(8,128)(2,1)} async-done(((bf16[768,768]{1,0:T(8,128)(2,1)}), bf16[192,768]{1,0:T(8,128)(2,1)}) %reduce-scatter.23.cloned.1.call-update) | async-done | bytes 294928 | tf_op jit(solution)/shard_map/reduce_scatter | solution.py:44
  701.2 20.3 %reduce-scatter.37.cloned.1.call-done = bf16[192,192]{1,0:T(8,128)(2,1)} async-done(((bf16[768,192]{1,0:T(8,128)(2,1)}), bf16[192,192]{1,0:T(8,128)(2,1)}) %reduce-scatter.37.cloned.1.call-update) | async-done | bytes 73744
  722.5 20.9 %reduce-scatter.35.cloned.1.call-done = bf16[192,192]{1,0:T(8,128)(2,1)} async-done(((bf16[768,192]{1,0:T(8,128)(2,1)}), bf16[192,192]{1,0:T(8,128)(2,1)}) %reduce-scatter.35.cloned.1.call-update) | async-done | bytes 73744
  745.0 25.0 %reduce-scatter.31.cloned.1.call-done = bf16[192,576]{1,0:T(8,128)(2,1)} async-done(((bf16[768,576]{1,0:T(8,128)(2,1)}), bf16[192,576]{1,0:T(8,128)(2,1)}) %reduce-scatter.31.cloned.1.call-update) | async-done | bytes 221200
  771.5 26.2 %reduce-scatter.33.cloned.1.call-done = bf16[192,576]{1,0:T(8,128)(2,1)} async-done(((bf16[768,576]{1,0:T(8,128)(2,1)}), bf16[192,576]{1,0:T(8,128)(2,1)}) %reduce-scatter.33.cloned.1.call-update) | async-done | bytes 221200
  800.1 4.2 bitcast_convert_fusion.1
  804.3 2.6 bitcast_convert_fusion
  807.0 1.9 copy-done.14
  812.6 3.9 pad_maximum_fusion.1
  821.3 40.8 %all-reduce = (f32[2,768]{1,0:T(2,128)S(1)}, f32[768]{0:T(1024)}, f32[3072]{0:T(1024)S(1)}, f32[768]{0:T(1024)}, f32[2,768]{1,0:T(2,128)}, /*index=5*/f32[2,768]{1,0:T(2,128)}) all-reduce(f32[2,768]{1,0:T(2,128)S(1)} %add.345, f32[768]{0:T(1024)S(1)} %add.348, ...), channel_id=1, replica_groups=mesh['fsdp'=4,'ctx'=2,'tp'=4] {'fsdp','ctx','tp'}, use_global_device_ids=true, to_apply=%region_43.44 | all-reduce | flops 9216 | bytes 73728 | tf_op jit(solution)/shard_map/psum | solution.py:275
  865.0 1.9 copy.57
  870.6 41.1 %all-reduce.12.cloned.1.call-done = (bf16[1024,768]{1,0:T(8,128)(2,1)}, bf16[1024,768]{1,0:T(8,128)(2,1)}) async-done(((bf16[1024,768]{1,0:T(8,128)(2,1)}, bf16[1024,768]{1,0:T(8,128)(2,1)}), (bf16[1024,768]{1,0:T(8,128)(2,1)}, bf16[1024,768]{1,0:T(8,128)(2,1)})) %all-reduce.12.cloned.1.call-update) | async-done | bytes 3145744 | tf_op jit(solution)/shard_map/psum | solution.py:253
  911.7 1.9 convert_add_fusion.2
  914.9 3.2 pad_maximum_fusion
  (439 shorter events, 112.7 us)
Async XLA Ops:
  8.0 67.3 %all-gather.5.cloned.1.call-start = ((), (), s32[]{:S(2)}) async-start(), calls=%async_computation.10 | async-start | bytes 2359296 | tf_op jit(solution)/shard_map/all_gather | solution.py:146
  44.2 151.0 %copy-start.18 = (bf16[2,512,768]{2,1,0:T(8,128)(2,1)}, bf16[2,512,768]{2,1,0:T(8,128)(2,1)S(1)}, u32[]{:S(2)}) copy-start(bf16[2,512,768]{2,1,0:T(8,128)(2,1)S(1)} %get-tuple-element.119) | copy-start | bytes 4718596
  44.2 151.0 %copy-start.20 = (bf16[2,512,768]{2,1,0:T(8,128)(2,1)}, bf16[2,512,768]{2,1,0:T(8,128)(2,1)S(1)}, u32[]{:S(2)}) copy-start(bf16[2,512,768]{2,1,0:T(8,128)(2,1)S(1)} %get-tuple-element.118) | copy-start | bytes 4718596
  47.1 42.4 %all-gather.11.cloned.1.call-start = ((), (), s32[]{:S(2)}) async-start(), calls=%async_computation.13 | async-start | bytes 2359296 | tf_op jit(solution)/shard_map/all_gather | solution.py:146
  50.1 4.9 copy-start.90
  50.1 9.8 %copy-start.61 = (bf16[192,192]{1,0:T(8,128)(2,1)S(1)}, bf16[192,192]{1,0:T(8,128)(2,1)}, u32[]{:S(2)}) copy-start(bf16[192,192]{1,0:T(8,128)(2,1)} %param.17) | copy-start | bytes 221188
  51.4 143.8 %all-reduce.18.cloned.1.call-start = ((), (), s32[]{:S(2)}) async-start(), calls=%async_computation.27 | async-start | bytes 6291456 | tf_op jit(solution)/shard_map/psum | solution.py:171
  76.9 5.9 copy-start.42
  76.9 8.6 copy-start.49
  91.1 5.5 copy-start.38
  91.1 8.2 copy-start.47
  106.4 98.1 %all-gather.7.cloned.1.call-start = ((), (), s32[]{:S(2)}) async-start(), calls=%async_computation.11 | async-start | bytes 1474560 | tf_op jit(solution)/shard_map/all_gather | solution.py:31
  107.0 119.1 %all-gather.9.cloned.1.call-start = ((), (), s32[]{:S(2)}) async-start(), calls=%async_computation.12 | async-start | bytes 1474560 | tf_op jit(solution)/shard_map/all_gather | solution.py:32
  107.5 212.7 %all-reduce.16.cloned.1.call-start = ((), (), s32[]{:S(2)}) async-start(), calls=%async_computation.26 | async-start | bytes 6291456 | tf_op jit(solution)/shard_map/psum | solution.py:179
  204.5 4.6 copy-start.4
  204.5 4.6 copy-start.64
  204.5 4.6 copy-start.67
  204.5 4.6 copy-start.91
  204.5 4.6 copy-start.109
  204.5 4.6 copy-start.113
  226.0 4.5 copy-start.111
  226.0 4.5 copy-start.119
  233.2 207.1 %all-reduce.14.cloned.1.call-start = ((), (), s32[]{:S(2)}) async-start(), calls=%async_computation.25 | async-start | bytes 6291456 | tf_op jit(solution)/shard_map/psum | solution.py:202
  335.4 4.8 copy-start.121
  335.4 5.8 copy-start.122
  337.6 4.5 copy-start.116
  337.6 5.4 copy-start.120
  343.0 5.0 copy-start.110
  353.2 268.8 %reduce-scatter.19.cloned.1.call-start = ((), (), s32[]{:S(2)}) async-start(), calls=%async_computation.14 | async-start | bytes 2359296 | tf_op jit(solution)/shard_map/reduce_scatter | solution.py:237
  440.3 7.9 copy-start.79
  440.3 7.9 copy-start.77
  440.3 7.9 copy-start.5
  440.3 7.9 copy-start.7
  440.3 7.9 copy-start.9
  440.3 7.9 copy-start.22
  440.3 8.3 copy-start.23
  440.3 8.3 copy-start.65
  440.3 8.3 copy-start.66
  440.3 8.2 copy-start.68
  440.3 8.2 copy-start.70
  440.4 8.2 copy-start.72
  453.5 6.7 slice-start
  455.9 9.8 %slice-start.2 = ((s8[6291456]{0:T(1024)(128)(4,1)}), s8[4194304]{0:T(1024)(128)(4,1)S(1)}, s32[]{:S(2)}) async-start(s8[6291456]{0:T(1024)(128)(4,1)} %bitcast.243), calls=%async_computation.31 | async-start | bytes 8388608
  460.2 5.6 slice-start.3
  506.8 156.9 %reduce-scatter.21.cloned.1.call-start = ((), (), s32[]{:S(2)}) async-start(), calls=%async_computation.15 | async-start | bytes 2359296 | tf_op jit(solution)/shard_map/reduce_scatter | solution.py:237
  565.9 108.1 %reduce-scatter.29.cloned.1.call-start = ((), (), s32[]{:S(2)}) async-start(), calls=%async_computation.19 | async-start | bytes 1474560 | tf_op jit(solution)/shard_map/reduce_scatter | solution.py:47
  570.3 4.8 copy-start.92
  570.3 103.7 %reduce-scatter.27.cloned.1.call-start = ((), (), s32[]{:S(2)}) async-start(), calls=%async_computation.18 | async-start | bytes 1474560 | tf_op jit(solution)/shard_map/reduce_scatter | solution.py:47
  575.1 100.8 %reduce-scatter.25.cloned.1.call-start = ((), (), s32[]{:S(2)}) async-start(), calls=%async_computation.17 | async-start | bytes 1474560 | tf_op jit(solution)/shard_map/reduce_scatter | solution.py:44
  580.2 119.2 %reduce-scatter.23.cloned.1.call-start = ((), (), s32[]{:S(2)}) async-start(), calls=%async_computation.16 | async-start | bytes 1474560 | tf_op jit(solution)/shard_map/reduce_scatter | solution.py:44
  584.3 4.5 copy-start.43
  584.3 137.1 %reduce-scatter.37.cloned.1.call-start = ((), (), s32[]{:S(2)}) async-start(), calls=%async_computation.23 | async-start | bytes 491520
  587.4 156.0 %reduce-scatter.35.cloned.1.call-start = ((), (), s32[]{:S(2)}) async-start(), calls=%async_computation.22 | async-start | bytes 491520
  588.9 15.9 %copy-start.41 = (bf16[1,1,1024,192]{2,3,1,0:T(8,128)(2,1)S(1)}, bf16[1,1,1024,192]{2,3,1,0:T(8,128)(2,1)}, u32[]{:S(2)}) copy-start(bf16[1,1,1024,192]{2,3,1,0:T(8,128)(2,1)} %copy-done.40) | copy-start | bytes 1179652
  620.7 149.4 %reduce-scatter.31.cloned.1.call-start = ((), (), s32[]{:S(2)}) async-start(), calls=%async_computation.20 | async-start | bytes 1228800
  623.3 176.9 %copy-start.32 = (bf16[3,1024,192]{1,2,0:T(8,128)(2,1)}, bf16[3,1024,192]{1,2,0:T(8,128)(2,1)S(1)}, u32[]{:S(2)}) copy-start(bf16[3,1024,192]{1,2,0:T(8,128)(2,1)S(1)} %constant_dynamic-update-slice_fusion) | copy-start | bytes 3538948
  625.3 4.9 copy-start.39
  630.1 16.3 %copy-start.37 = (bf16[1,1,1024,192]{2,3,1,0:T(8,128)(2,1)S(1)}, bf16[1,1,1024,192]{2,3,1,0:T(8,128)(2,1)}, u32[]{:S(2)}) copy-start(bf16[1,1,1024,192]{2,3,1,0:T(8,128)(2,1)} %copy-done.36) | copy-start | bytes 1179652
  630.1 167.5 %reduce-scatter.33.cloned.1.call-start = ((), (), s32[]{:S(2)}) async-start(), calls=%async_computation.21 | async-start | bytes 1228800
  673.9 189.5 %all-reduce.20.cloned.1.call-start = ((), (), s32[]{:S(2)}) async-start(), calls=%async_computation.28 | async-start | bytes 1966080 | tf_op jit(solution)/shard_map/psum | solution.py:270
  799.9 111.8 %all-reduce.12.cloned.1.call-start = ((), (), s32[]{:S(2)}) async-start(), calls=%async_computation.24 | async-start | bytes 6291456 | tf_op jit(solution)/shard_map/psum | solution.py:253
  807.0 5.2 copy-start.105
  812.5 6.6 copy-start.33
  816.7 95.0 %copy-start.12 = (f32[1024,768]{1,0:T(8,128)S(1)}, f32[1024,768]{1,0:T(8,128)}, u32[]{:S(2)}) copy-start(f32[1024,768]{1,0:T(8,128)} %copy-done.11) | copy-start | bytes 9437188
  (82 other events, 217.5 us)
Sparse Core Ops, SparseCore 0:
  47.2 11.1 all-gather.4
  60.0 10.9 all-gather.10
  106.5 88.5 all-reduce.17
  233.3 86.9 all-reduce.15
  353.3 86.9 all-reduce.13
  506.9 8.9 reduce-scatter.18
  566.0 8.9 reduce-scatter.20
  577.3 30.6 reduce-scatter.28
  610.3 27.9 reduce-scatter.26
  640.5 27.9 reduce-scatter.24
  671.4 27.8 reduce-scatter.22
  702.0 19.3 reduce-scatter.36
  724.3 19.0 reduce-scatter.34
  745.6 24.4 reduce-scatter.30
  772.8 24.8 reduce-scatter.32
  801.3 18.0 all-reduce.19
  822.9 88.7 all-reduce.11
Sparse Core Ops, SparseCore 1:
  108.4 31.7 all-gather.6
  141.6 29.3 all-gather.8
where the time goes:
time: 932 us; the launch traced here: 925 us
  waiting for transfers between devices  410 us (44%)
  matrix products  257 us (28%)
  blocking collectives  86.9 us (9%)
  other arithmetic  86.7 us (9%)
  local copies, waits for them, and re-layouts  66 us (7%)
  between operations  17.3 us (2%)
    unnamed x23, waiting for transfers between devices  93.8 us
    psum x1, waiting for transfers between devices, per_device(): lax.psum(attn_part.astype(jnp.bfloat16), 'tp').astype(jnp.float32)  86.1 us
    psum x1, waiting for transfers between devices, per_device(): lax.psum(branch_part.astype(jnp.bfloat16), 'tp').astype(jnp.float32)  83.8 us
    psum x1, waiting for transfers between devices, per_device(): lax.psum(normed_part.astype(jnp.bfloat16), 'tp').astype(jnp.float32)  81.8 us
    dot_general x4, matrix products, attend_back(): jnp.einsum('hqk,qhd->khd', grad_scores, queries, preferred_element_type=j...  72.7 us
    dot_general x4, matrix products, attend_back(): jnp.einsum('hqk,khd->qhd', grad_scores, keys_all, preferred_element_type=...  63.6 us
    unnamed x275, local copies, waits for them, and re-layouts  43.2 us
    psum x1, waiting for transfers between devices, per_device(): lax.psum(input_part.astype(jnp.bfloat16), 'tp').astype(jnp.float32)  41.1 us
  transfers between devices with their start and end apart: 19, of which 9 were waited for; matrix products, arithmetic and copies ran while one was open for 28% of the time, Pallas kernels for 0%

commit v1 on v0

v1 whole, which is shorter than its diff:
```python
import functools
import math

import jax
import jax.numpy as jnp
from jax import lax
from jax.experimental import pallas as pl
from jax.experimental.pallas import tpu as pltpu
from jax.sharding import PartitionSpec as P

HD = 64
EPS = 1e-05
MASKED = -1000000000.0
LOG2E = math.log2(math.e)
SCALE = 0.125
BF = jnp.bfloat16
F32 = jnp.float32
VMEM_LIMIT = 60 * 1024 * 1024

X_SWAP = [(0, 1), (1, 0), (2, 3), (3, 2)]
Y_SWAP = [(0, 2), (2, 0), (1, 3), (3, 1)]
C_SWAP = [(0, 1), (1, 0)]


def nn(a, b):
    return lax.dot_general(a, b, (((1,), (0,)), ((), ())), preferred_element_type=F32)


def nt(a, b):
    return lax.dot_general(a, b, (((1,), (1,)), ((), ())), preferred_element_type=F32)


def tn(a, b):
    return lax.dot_general(a, b, (((0,), (0,)), ((), ())), preferred_element_type=F32)


def params(n=1):
    return pltpu.CompilerParams(
        dimension_semantics=("arbitrary",) * n, vmem_limit_bytes=VMEM_LIMIT
    )


def cost(flops, moved, trans=0):
    return pl.CostEstimate(flops=int(flops), bytes_accessed=int(moved), transcendentals=int(trans))


def spec(shape, index):
    return pl.BlockSpec(shape, index)


def whole(shape):
    zeros = (0,) * len(shape)
    return pl.BlockSpec(shape, lambda i, info: zeros)


def qkv_kernel(info, x_ref, a_ref, qb_ref, kvb_ref, q_ref, kv_ref):
    c = info[0]
    x = x_ref[...]
    kv_ref[0] = (nn(x, a_ref[c, 0]) + kvb_ref[0]).astype(BF)
    q_ref[0] = (nn(x, a_ref[1 - c, 0, :, 0 : q_ref.shape[2]]) + qb_ref[0]).astype(BF)


def qkv_call(info, x, wa, qb, kvb):
    rows, width = x.shape
    slots, half = wa.shape[1], wa.shape[3]
    feat = half // 2
    return pl.pallas_call(
        qkv_kernel,
        grid_spec=pltpu.PrefetchScalarGridSpec(
            num_scalar_prefetch=1,
            grid=(slots,),
            in_specs=[
                whole((rows, width)),
                spec((2, 1, width, half), lambda i, info: (0, i, 0, 0)),
                spec((1, 1, feat), lambda i, info: (i, 0, 0)),
                spec((1, 1, half), lambda i, info: (i, 0, 0)),
            ],
            out_specs=[
                spec((1, rows, feat), lambda i, info: (i, 0, 0)),
                spec((1, rows, half), lambda i, info: (i, 0, 0)),
            ],
        ),
        out_shape=[
            jax.ShapeDtypeStruct((slots, rows, feat), BF),
            jax.ShapeDtypeStruct((slots, rows, half), BF),
        ],
        compiler_params=params(),
        cost_estimate=cost(2 * rows * width * slots * 3 * feat, 8e6),
        name="qkv",
    )(info, x, wa, qb, kvb)


CHUNK = 256


def key_bias(info, rows, mine):
    owner = info[0] if mine else 1 - info[0]
    position = owner * rows + lax.broadcasted_iota(jnp.int32, (1, rows), 1)
    return jnp.where(position < info[1], 0.0, MASKED)


def attn_kernel(info, q_ref, kv_ref, kvo_ref, ctx_ref, lse_ref):
    rows, feat = q_ref.shape[1], q_ref.shape[2]
    heads = feat // HD
    bias_m, bias_o = key_bias(info, rows, True), key_bias(info, rows, False)
    step_rows = min(CHUNK, rows)
    lane = lax.broadcasted_iota(jnp.int32, (1, 128), 1)

    def chunk(n, carry):
        at = pl.ds(pl.multiple_of(n * step_rows, step_rows), step_rows)
        lse_all = jnp.zeros((step_rows, 128), F32)
        for h in range(heads):
            cols = slice(h * HD, (h + 1) * HD)
            vcols = slice(feat + h * HD, feat + (h + 1) * HD)
            q = q_ref[0, at, cols]
            s_m = nt(q, kv_ref[0, :, cols]) * (SCALE * LOG2E) + bias_m
            s_o = nt(q, kvo_ref[0, :, cols]) * (SCALE * LOG2E) + bias_o
            top = jnp.maximum(
                jnp.max(s_m, axis=1, keepdims=True), jnp.max(s_o, axis=1, keepdims=True)
            )
            e_m = jnp.exp2(s_m - top)
            e_o = jnp.exp2(s_o - top)
            total = jnp.sum(e_m, axis=1, keepdims=True) + jnp.sum(e_o, axis=1, keepdims=True)
            inv = 1.0 / total
            out = nn((e_m * inv).astype(BF), kv_ref[0, :, vcols]) + nn(
                (e_o * inv).astype(BF), kvo_ref[0, :, vcols]
            )
            ctx_ref[0, at, cols] = out.astype(BF)
            lse_all = jnp.where(lane == h, top + jnp.log2(total), lse_all)
        lse_ref[0, at, :] = lse_all
        return carry

    lax.fori_loop(0, rows // step_rows, chunk, 0)


def attn_call(info, q, kv, kvo):
    slots, rows, feat = q.shape
    half = kv.shape[2]
    blk = lambda w: spec((1, rows, w), lambda i, info: (i, 0, 0))
    heads = slots * feat // HD
    return pl.pallas_call(
        attn_kernel,
        grid_spec=pltpu.PrefetchScalarGridSpec(
            num_scalar_prefetch=1,
            grid=(slots,),
            in_specs=[blk(feat), blk(half), blk(half)],
            out_specs=[blk(feat), blk(128)],
        ),
        out_shape=[
            jax.ShapeDtypeStruct((slots, rows, feat), BF),
            jax.ShapeDtypeStruct((slots, rows, 128), F32),
        ],
        compiler_params=params(),
        cost_estimate=cost(
            16 * rows * rows * 2 * HD * heads, 8e6, 2 * rows * rows * heads
        ),
        name="attn",
    )(info, q, kv, kvo)


def attn_back_kernel(info, q_ref, kv_ref, kvo_ref, lse_ref, g_ref, gq_ref, gkv_ref, gkvo_ref, acc_m, acc_o):
    rows, feat = q_ref.shape[1], q_ref.shape[2]
    heads = feat // HD
    bias_m, bias_o = key_bias(info, rows, True), key_bias(info, rows, False)
    step_rows = min(CHUNK, rows)
    lane = lax.broadcasted_iota(jnp.int32, (1, 128), 1)
    acc_m[...] = jnp.zeros_like(acc_m)
    acc_o[...] = jnp.zeros_like(acc_o)

    def chunk(n, carry):
        at = pl.ds(pl.multiple_of(n * step_rows, step_rows), step_rows)
        lse_all = lse_ref[0, at, :]
        for h in range(heads):
            cols = slice(h * HD, (h + 1) * HD)
            vcols = slice(feat + h * HD, feat + (h + 1) * HD)
            q = q_ref[0, at, cols]
            g = g_ref[0, at, cols]
            lse = jnp.sum(jnp.where(lane == h, lse_all, 0.0), axis=1, keepdims=True)
            k_m, k_o = kv_ref[0, :, cols], kvo_ref[0, :, cols]
            p_m = jnp.exp2(nt(q, k_m) * (SCALE * LOG2E) + bias_m - lse)
            p_o = jnp.exp2(nt(q, k_o) * (SCALE * LOG2E) + bias_o - lse)
            gp_m = nt(g, kv_ref[0, :, vcols])
            gp_o = nt(g, kvo_ref[0, :, vcols])
            inner = jnp.sum(p_m * gp_m, axis=1, keepdims=True) + jnp.sum(
                p_o * gp_o, axis=1, keepdims=True
            )
            acc_m[:, vcols] += tn(p_m.astype(BF), g)
            acc_o[:, vcols] += tn(p_o.astype(BF), g)
            gs_m = (p_m * (gp_m - inner) * SCALE).astype(BF)
            gs_o = (p_o * (gp_o - inner) * SCALE).astype(BF)
            gq_ref[0, at, cols] = (nn(gs_m, k_m) + nn(gs_o, k_o)).astype(BF)
            acc_m[:, cols] += tn(gs_m, q)
            acc_o[:, cols] += tn(gs_o, q)
        return carry

    lax.fori_loop(0, rows // step_rows, chunk, 0)
    gkv_ref[0] = acc_m[...]
    gkvo_ref[0] = acc_o[...].astype(BF)


def attn_back_call(info, q, kv, kvo, lse, g):
    slots, rows, feat = q.shape
    half = kv.shape[2]
    blk = lambda w: spec((1, rows, w), lambda i, info: (i, 0, 0))
    heads = slots * feat // HD
    return pl.pallas_call(
        attn_back_kernel,
        grid_spec=pltpu.PrefetchScalarGridSpec(
            num_scalar_prefetch=1,
            grid=(slots,),
            in_specs=[blk(feat), blk(half), blk(half), blk(128), blk(feat)],
            out_specs=[blk(feat), blk(half), blk(half)],
            scratch_shapes=[pltpu.VMEM((rows, half), F32), pltpu.VMEM((rows, half), F32)],
        ),
        out_shape=[
            jax.ShapeDtypeStruct((slots, rows, feat), BF),
            jax.ShapeDtypeStruct((slots, rows, half), F32),
            jax.ShapeDtypeStruct((slots, rows, half), BF),
        ],
        compiler_params=params(),
        cost_estimate=cost(
            40 * rows * rows * 2 * HD * heads, 12e6, 2 * rows * rows * heads
        ),
        name="attn_back",
    )(info, q, kv, kvo, lse, g)


ROWS = 128


def row_mask(info, rows, start, count):
    position = info[0] * rows + start + lax.broadcasted_iota(jnp.int32, (count, 1), 0)
    return (position < info[1]).astype(F32)


def ffn_kernel(
    info, ctx_ref, wo_ref, x_ref, cot_ref, vec_ref, bin_ref, wb_ref, wc_ref,
    act_ref, slope_ref, nlow_ref, hat_ref, rstd_ref, out_ref, gb_ref, gr_ref, sums_ref,
    normed_sc, branch_sc,
):
    k = pl.program_id(0)
    rows, width = x_ref.shape
    slots, feat = ctx_ref.shape[0], ctx_ref.shape[2]

    @pl.when(k == 0)
    def _():
        def chunk(n, carry):
            at = pl.ds(pl.multiple_of(n * ROWS, ROWS), ROWS)
            res = x_ref[at, :].astype(F32) + vec_ref[0:1, :]
            for s in range(slots):
                res += nt(ctx_ref[s, at, :], wo_ref[0, s, :, feat : 2 * feat])
            center = jnp.mean(res, axis=1, keepdims=True)
            res = res - center
            rstd = lax.rsqrt(jnp.mean(res * res, axis=1, keepdims=True) + EPS)
            hat = res * rstd
            normed = hat * vec_ref[2:3, :] + vec_ref[4:5, :]
            hat_ref[at, :] = hat
            rstd_ref[at, :] = jnp.broadcast_to(rstd, (ROWS, 128))
            normed_sc[at, :] = normed
            nlow_ref[at, :] = normed.astype(BF)
            return carry

        lax.fori_loop(0, rows // ROWS, chunk, 0)

    def chunk(n, carry):
        at = pl.ds(pl.multiple_of(n * ROWS, ROWS), ROWS)
        u = nn(nlow_ref[at, :], wb_ref[0]) + bin_ref[0]
        cdf = 0.5 + 0.5 * lax.erf(u * math.sqrt(0.5))
        act = (u * cdf).astype(BF)
        act_ref[0, at, :] = act
        slope_ref[0, at, :] = cdf + u * (jnp.exp(u * u * -0.5) * (1.0 / math.sqrt(2.0 * math.pi)))
        part = nt(act, wc_ref[0])

        @pl.when(k == 0)
        def _():
            branch_sc[at, :] = part

        @pl.when(k > 0)
        def _():
            branch_sc[at, :] += part

        return carry

    lax.fori_loop(0, rows // ROWS, chunk, 0)

    @pl.when(k == pl.num_programs(0) - 1)
    def _():
        def chunk(n, carry):
            s_gain, s_shift, s_bias = carry
            at = pl.ds(pl.multiple_of(n * ROWS, ROWS), ROWS)
            res = normed_sc[at, :] + branch_sc[at, :] + vec_ref[1:2, :]
            center = jnp.mean(res, axis=1, keepdims=True)
            res = res - center
            rstd = lax.rsqrt(jnp.mean(res * res, axis=1, keepdims=True) + EPS)
            hat = res * rstd
            out_ref[at, :] = (hat * vec_ref[3:4, :] + vec_ref[5:6, :]).astype(BF)
            g = cot_ref[at, :].astype(F32) * row_mask(info, rows, n * ROWS, ROWS)
            s_shift += jnp.sum(g, axis=0, keepdims=True)
            s_gain += jnp.sum(g * hat, axis=0, keepdims=True)
            gh = g * vec_ref[3:4, :]
            gr = rstd * (
                gh
                - jnp.mean(gh, axis=1, keepdims=True)
                - hat * jnp.mean(gh * hat, axis=1, keepdims=True)
            )
            gr_ref[at, :] = gr
            gb = gr.astype(BF)
            gb_ref[at, :] = gb
            s_bias += jnp.sum(gb.astype(F32), axis=0, keepdims=True)
            return s_gain, s_shift, s_bias

        zero = jnp.zeros((1, width), F32)
        s_gain, s_shift, s_bias = lax.fori_loop(0, rows // ROWS, chunk, (zero, zero, zero))
        sums_ref[0:1, :] = s_gain
        sums_ref[1:2, :] = s_shift
        sums_ref[2:3, :] = s_bias
        sums_ref[3:8, :] = jnp.zeros((5, width), F32)


def ffn_call(info, ctx, wa, x, cot, vec, b_in, wb, wc):
    slots, rows, feat = ctx.shape
    width = x.shape[1]
    blocks, _, half = wb.shape
    kblk = lambda r, w: spec((1, r, w), lambda i, info: (i, 0, 0))
    return pl.pallas_call(
        ffn_kernel,
        grid_spec=pltpu.PrefetchScalarGridSpec(
            num_scalar_prefetch=1,
            grid=(blocks,),
            in_specs=[
                whole((slots, rows, feat)),
                spec((1, slots, width, half), lambda i, info: (1 - info[0], 0, 0, 0)),
                whole((rows, width)),
                whole((rows, width)),
                whole((8, width)),
                kblk(1, half),
                kblk(width, half),
                kblk(width, half),
            ],
            out_specs=[
                kblk(rows, half),
                kblk(rows, half),
                whole((rows, width)),
                whole((rows, width)),
                whole((rows, 128)),
                whole((rows, width)),
                whole((rows, width)),
                whole((rows, width)),
                whole((8, width)),
            ],
            scratch_shapes=[pltpu.VMEM((rows, width), F32), pltpu.VMEM((rows, width), F32)],
        ),
        out_shape=[
            jax.ShapeDtypeStruct((blocks, rows, half), BF),
            jax.ShapeDtypeStruct((blocks, rows, half), F32),
            jax.ShapeDtypeStruct((rows, width), BF),
            jax.ShapeDtypeStruct((rows, width), F32),
            jax.ShapeDtypeStruct((rows, 128), F32),
            jax.ShapeDtypeStruct((rows, width), BF),
            jax.ShapeDtypeStruct((rows, width), BF),
            jax.ShapeDtypeStruct((rows, width), F32),
            jax.ShapeDtypeStruct((8, width), F32),
        ],
        compiler_params=params(),
        cost_estimate=cost(4 * rows * width * blocks * half * 3, 3e7, 2 * rows * blocks * half),
        name="ffn",
    )(info, ctx, wa, x, cot, vec, b_in, wb, wc)


def down_kernel(info, gb_ref, act_ref, dc_ref, gt_sc):
    @pl.when(pl.program_id(0) == 0)
    def _():
        gt_sc[...] = gb_ref[...].T

    dc_ref[0] = nn(gt_sc[...], act_ref[0]).astype(BF)


def down_call(info, gb, act):
    rows, width = gb.shape
    blocks, _, half = act.shape
    kblk = lambda r, w: spec((1, r, w), lambda i, info: (i, 0, 0))
    return pl.pallas_call(
        down_kernel,
        grid_spec=pltpu.PrefetchScalarGridSpec(
            num_scalar_prefetch=1,
            grid=(blocks,),
            in_specs=[whole((rows, width)), kblk(rows, half)],
            out_specs=kblk(width, half),
            scratch_shapes=[pltpu.VMEM((width, rows), BF)],
        ),
        out_shape=jax.ShapeDtypeStruct((blocks, width, half), BF),
        compiler_params=params(),
        cost_estimate=cost(2 * rows * width * blocks * half, 9e6),
        name="down_grad",
    )(info, gb, act)


def ffn_back_kernel(
    info, gb_ref, slope_ref, wc_ref, wb_ref, nlow_ref, gr_ref, hat_ref, rstd_ref, vec_ref, wo_ref, ctx_ref,
    db_ref, dbin_ref, g1_ref, gatt_ref, gctx_ref, dwo_ref, sums_ref,
    nt_sc, acc_sc, gh_sc,
):
    k = pl.program_id(0)
    rows, width = gb_ref.shape
    half = wb_ref.shape[2]
    slots, feat = ctx_ref.shape[0], ctx_ref.shape[2]

    @pl.when(k == 0)
    def _():
        nt_sc[...] = nlow_ref[...].T

    def chunk(n, total):
        at = pl.ds(pl.multiple_of(n * ROWS, ROWS), ROWS)
        gh = (slope_ref[0, at, :] * nn(gb_ref[at, :], wc_ref[0])).astype(BF)
        gh_sc[at, :] = gh
        part = nt(gh, wb_ref[0])

        @pl.when(k == 0)
        def _():
            acc_sc[at, :] = part

        @pl.when(k > 0)
        def _():
            acc_sc[at, :] += part

        return total + jnp.sum(gh.astype(F32), axis=0, keepdims=True)

    dbin_ref[0] = lax.fori_loop(0, rows // ROWS, chunk, jnp.zeros((1, half), F32))
    db_ref[0] = nn(nt_sc[...], gh_sc[...]).astype(BF)

    @pl.when(k == pl.num_programs(0) - 1)
    def _():
        def chunk(n, carry):
            s_gain, s_shift, s_bias = carry
            at = pl.ds(pl.multiple_of(n * ROWS, ROWS), ROWS)
            g = acc_sc[at, :] + gr_ref[at, :]
            hat = hat_ref[at, :]
            s_shift += jnp.sum(g, axis=0, keepdims=True)
            s_gain += jnp.sum(g * hat, axis=0, keepdims=True)
            gh = g * vec_ref[2:3, :]
            g1 = rstd_ref[at, 0:1] * (
                gh
                - jnp.mean(gh, axis=1, keepdims=True)
                - hat * jnp.mean(gh * hat, axis=1, keepdims=True)
            )
            g1_ref[at, :] = g1
            gatt = g1.astype(BF)
            gatt_ref[at, :] = gatt
            s_bias += jnp.sum(gatt.astype(F32), axis=0, keepdims=True)
            for s in range(slots):
                gctx_ref[s, at, :] = nn(gatt, wo_ref[0, s, :, feat : 2 * feat]).astype(BF)
            return s_gain, s_shift, s_bias

        zero = jnp.zeros((1, width), F32)
        s_gain, s_shift, s_bias = lax.fori_loop(0, rows // ROWS, chunk, (zero, zero, zero))
        sums_ref[0:1, :] = s_gain
        sums_ref[1:2, :] = s_shift
        sums_ref[2:3, :] = s_bias
        sums_ref[3:8, :] = jnp.zeros((5, width), F32)
        nt_sc[...] = gatt_ref[...].T
        for s in range(slots):
            dwo_ref[s] = nn(nt_sc[...], ctx_ref[s]).astype(BF)


def ffn_back_call(info, gb, slope, wc, wb, nlow, gr, hat, rstd, vec, wa, ctx):
    slots, rows, feat = ctx.shape
    width = gb.shape[1]
    blocks, _, half = wb.shape
    kblk = lambda r, w: spec((1, r, w), lambda i, info: (i, 0, 0))
    return pl.pallas_call(
        ffn_back_kernel,
        grid_spec=pltpu.PrefetchScalarGridSpec(
            num_scalar_prefetch=1,
            grid=(blocks,),
            in_specs=[
                whole((rows, width)),
                kblk(rows, half),
                kblk(width, half),
                kblk(width, half),
                whole((rows, width)),
                whole((rows, width)),
                whole((rows, width)),
                whole((rows, 128)),
                whole((8, width)),
                spec((1, slots, width, half), lambda i, info: (1 - info[0], 0, 0, 0)),
                whole((slots, rows, feat)),
            ],
            out_specs=[
                kblk(width, half),
                kblk(1, half),
                whole((rows, width)),
                whole((rows, width)),
                whole((slots, rows, feat)),
                whole((slots, width, feat)),
                whole((8, width)),
            ],
            scratch_shapes=[
                pltpu.VMEM((width, rows), BF),
                pltpu.VMEM((rows, width), F32),
                pltpu.VMEM((rows, half), BF),
            ],
        ),
        out_shape=[
            jax.ShapeDtypeStruct((blocks, width, half), BF),
            jax.ShapeDtypeStruct((blocks, 1, half), F32),
            jax.ShapeDtypeStruct((rows, width), F32),
            jax.ShapeDtypeStruct((rows, width), BF),
            jax.ShapeDtypeStruct((slots, rows, feat), BF),
            jax.ShapeDtypeStruct((slots, width, feat), BF),
            jax.ShapeDtypeStruct((8, width), F32),
        ],
        compiler_params=params(),
        cost_estimate=cost(6 * rows * width * blocks * half, 3e7),
        name="ffn_back",
    )(info, gb, slope, wc, wb, nlow, gr, hat, rstd, vec, wa, ctx)


def qkv_back_kernel(
    info, x_ref, gq_ref, gkv_ref, gkvo_ref, wa_ref, dwo_ref, g1_ref,
    da_ref, gx_ref, sq_ref, skv_ref, xt_sc, acc_sc,
):
    s = pl.program_id(0)
    c = info[0]
    feat = gq_ref.shape[2]

    @pl.when(s == 0)
    def _():
        xt_sc[...] = x_ref[...].T
        acc_sc[...] = g1_ref[...]

    gkv = (gkv_ref[0] + gkvo_ref[0].astype(F32)).astype(BF)
    gq = gq_ref[0]
    da_ref[c, 0] = nn(xt_sc[...], gkv).astype(BF)
    da_ref[1 - c, 0, :, 0:feat] = nn(xt_sc[...], gq).astype(BF)
    da_ref[1 - c, 0, :, feat : 2 * feat] = dwo_ref[0]
    sq_ref[0] = jnp.sum(gq.astype(F32), axis=0, keepdims=True)
    skv_ref[0] = jnp.sum(gkv.astype(F32), axis=0, keepdims=True)
    acc_sc[...] += nt(gkv, wa_ref[c, 0]) + nt(gq, wa_ref[1 - c, 0, :, 0:feat])

    @pl.when(s == pl.num_programs(0) - 1)
    def _():
        gx_ref[...] = acc_sc[...].astype(BF)


def qkv_back_call(info, x, gq, gkv, gkvo, wa, dwo, g1):
    rows, width = x.shape
    slots, _, feat = gq.shape
    half = gkv.shape[2]
    blk = lambda r, w: spec((1, r, w), lambda i, info: (i, 0, 0))
    return pl.pallas_call(
        qkv_back_kernel,
        grid_spec=pltpu.PrefetchScalarGridSpec(
            num_scalar_prefetch=1,
            grid=(slots,),
            in_specs=[
                whole((rows, width)),
                blk(rows, feat),
                blk(rows, half),
                blk(rows, half),
                spec((2, 1, width, half), lambda i, info: (0, i, 0, 0)),
                blk(width, feat),
                whole((rows, width)),
            ],
            out_specs=[
                spec((2, 1, width, half), lambda i, info: (0, i, 0, 0)),
                whole((rows, width)),
                blk(1, feat),
                blk(1, half),
            ],
            scratch_shapes=[pltpu.VMEM((width, rows), BF), pltpu.VMEM((rows, width), F32)],
        ),
        out_shape=[
            jax.ShapeDtypeStruct((2, slots, width, half), BF),
            jax.ShapeDtypeStruct((rows, width), BF),
            jax.ShapeDtypeStruct((slots, 1, feat), F32),
            jax.ShapeDtypeStruct((slots, 1, half), F32),
        ],
        compiler_params=params(),
        cost_estimate=cost(4 * rows * width * slots * 3 * feat, 2e7),
        name="qkv_back",
    )(info, x, gq, gkv, gkvo, wa, dwo, g1)


def ring(size, step):
    return [(i, (i + step) % size) for i in range(size)]


def column_gather(shard, rank, size):
    if size > 4:
        return lax.all_gather(shard, "fsdp", axis=0, tiled=True)
    rows = shard.shape[0]
    full = jnp.zeros((size * rows,) + shard.shape[1:], shard.dtype)
    full = lax.dynamic_update_slice_in_dim(full, shard, rank * rows, 0)
    for step in range(1, size):
        got = lax.ppermute(shard, "fsdp", ring(size, step))
        full = lax.dynamic_update_slice_in_dim(full, got, ((rank - step) % size) * rows, 0)
    return full


def column_scatter(full, rank, size):
    rows = full.shape[0] // size
    if size > 4:
        return lax.psum_scatter(full, "fsdp", scatter_dimension=0, tiled=True).astype(F32)
    total = lax.dynamic_slice_in_dim(full, rank * rows, rows, 0).astype(F32)
    for step in range(1, size):
        piece = lax.dynamic_slice_in_dim(full, ((rank + step) % size) * rows, rows, 0)
        total = total + lax.ppermute(piece, "fsdp", ring(size, step)).astype(F32)
    return total


def plane_gather(mine):
    cut = mine.shape[0] // 2
    from_x = lax.ppermute(mine, "tp", X_SWAP)
    from_y = lax.ppermute(mine, "tp", Y_SWAP)
    upper = lax.ppermute(from_y[:cut], "tp", X_SWAP)
    lower = lax.ppermute(from_x[cut:], "tp", Y_SWAP)
    return mine, from_x, from_y, jnp.concatenate((upper, lower), axis=0)


def add(a, b):
    return (a.astype(F32) + b.astype(F32)).astype(BF)


def plane_scatter(blocks):
    cut = blocks.shape[1] // 2
    up, down = blocks[:, :cut], blocks[:, cut:]
    got = lax.ppermute(jnp.stack((up[1], up[3])), "tp", X_SWAP)
    mid_up = add(up[0], got[0])
    pass_up = add(up[2], got[1])
    got = lax.ppermute(jnp.stack((down[2], down[3])), "tp", Y_SWAP)
    mid_down = add(down[0], got[0])
    pass_down = add(down[1], got[1])
    upper = add(mid_up, lax.ppermute(pass_up, "tp", Y_SWAP))
    lower = add(mid_down, lax.ppermute(pass_down, "tp", X_SWAP))
    return jnp.concatenate((upper, lower), axis=0)


def weight_gather(shard, rank, size):
    column = column_gather(shard, rank, size)
    mine = jnp.stack(plane_gather(column))
    return jnp.stack((mine, lax.ppermute(mine, "ctx", C_SWAP)))


def weight_scatter(mine, other, rank, size):
    blocks = add(mine, lax.ppermute(other, "ctx", C_SWAP))
    return column_scatter(plane_scatter(blocks), rank, size).astype(BF)


def by_index(slots, index):
    swapped = jnp.where(index % 2 == 1, slots[jnp.array([1, 0, 3, 2])], slots)
    return jnp.where(index // 2 == 1, swapped[jnp.array([2, 3, 0, 1])], swapped)


def sum_everywhere(value, size):
    value = value + lax.ppermute(value, "ctx", C_SWAP)
    value = value + lax.ppermute(value, "tp", X_SWAP)
    value = value + lax.ppermute(value, "tp", Y_SWAP)
    step = 1
    while step < size:
        value = value + lax.ppermute(value, "fsdp", [(i, i ^ step) for i in range(size)])
        step *= 2
    return value


def place_sequences(slots, index, dtype):
    out = jnp.zeros((len(slots),) + slots[0].shape, dtype)
    for distance, block in enumerate(slots):
        out = lax.dynamic_update_slice(out, block.astype(dtype)[None], (index ^ distance, 0, 0))
    return out


def per_device(
    tokens, lengths, qkv_weight, qv_bias, out_weight, out_bias, ffn_in, ffn_in_bias,
    ffn_out, ffn_out_bias, norm_gains, norm_shifts, cotangent,
):
    size = lax.axis_size("fsdp")
    rank = lax.axis_index("fsdp")
    c = lax.axis_index("ctx")
    t = lax.axis_index("tp")
    seqs, rows, width = tokens.shape
    assert lax.axis_size("tp") == 4 and lax.axis_size("ctx") == 2 and seqs == 4
    feat = qkv_weight.shape[2]
    units = ffn_in.shape[1]
    half = units // 2
    assert half == 2 * feat
    x = lax.dynamic_index_in_dim(tokens, t, 0, keepdims=False)
    cot = lax.dynamic_index_in_dim(cotangent, t, 0, keepdims=False)
    length = lax.dynamic_index_in_dim(lengths, t, 0, keepdims=False)
    info = jnp.stack((c.astype(jnp.int32), length))

    shard_a = jnp.where(
        c == 0,
        jnp.concatenate((qkv_weight[1], qkv_weight[2]), axis=1),
        jnp.concatenate((qkv_weight[0], out_weight.T), axis=1),
    )
    shard_b = lax.dynamic_slice_in_dim(ffn_in, c * half, half, 1)
    shard_c = lax.dynamic_slice_in_dim(ffn_out, c * half, half, 0).T

    bias_own = jnp.concatenate((qv_bias.reshape(-1), ffn_in_bias)).reshape(1, -1)
    bias_x = lax.ppermute(bias_own, "tp", X_SWAP)
    bias_y = lax.ppermute(bias_own, "tp", Y_SWAP)
    bias_d = lax.ppermute(bias_x, "tp", Y_SWAP)
    bias = jnp.stack((bias_own, bias_x, bias_y, bias_d))
    q_bias = bias[:, :, :feat]
    kv_bias = jnp.concatenate((jnp.zeros_like(q_bias), bias[:, :, feat : 2 * feat]), axis=2)
    in_bias = bias[:, 0, 2 * feat :].reshape(4, 2, half).transpose(1, 0, 2)
    in_bias = jnp.where(c == 0, in_bias, in_bias[::-1]).reshape(8, 1, half)

    wa = weight_gather(shard_a, rank, size)
    wb = weight_gather(shard_b, rank, size).reshape(8, width, half)
    wc = weight_gather(shard_c, rank, size).reshape(8, width, half)
    zero_row = jnp.zeros_like(out_bias)
    vec = jnp.stack((out_bias, ffn_out_bias, norm_gains[0], norm_gains[1], norm_shifts[0], norm_shifts[1], zero_row, zero_row))

    q, kv = qkv_call(info, x, wa, q_bias, kv_bias)
    kv_other = lax.ppermute(kv, "ctx", C_SWAP)
    context, lse = attn_call(info, q, kv, kv_other)
    act, slope, nlow, hat, rstd, out, g_branch, g_r2, sums_two = ffn_call(
        info, context, wa, x, cot, vec, in_bias, wb, wc
    )
    layer_output = place_sequences(plane_gather(out), t, BF)
    dc = down_call(info, g_branch, act)
    own_c = weight_scatter(dc[:4], dc[4:], rank, size)
    db, d_in_bias, g_r1, g_att, g_context, dwo, sums_one = ffn_back_call(
        info, g_branch, slope, wc, wb, nlow, g_r2, hat, rstd, vec, wa, context
    )
    own_b = weight_scatter(db[:4], db[4:], rank, size)
    gq, gkv, gkv_send = attn_back_call(info, q, kv, kv_other, lse, g_context)
    gkv_got = lax.ppermute(gkv_send, "ctx", C_SWAP)
    da, g_tokens, sum_q, sum_kv = qkv_back_call(info, x, gq, gkv, gkv_got, wa, dwo, g_r1)
    own_a = weight_scatter(da[0], da[1], rank, size)
    grad_tokens = place_sequences(plane_gather(g_tokens), t, F32)

    own = jnp.stack((own_a, own_b, own_c))
    other = lax.ppermute(own, "ctx", C_SWAP)
    first = jnp.where(c == 0, own, other).astype(F32)
    second = jnp.where(c == 0, other, own).astype(F32)
    grad_qkv = jnp.stack((second[0][:, :feat], first[0][:, :feat], first[0][:, feat:]))
    grad_out = second[0][:, feat:].T
    grad_in = jnp.concatenate((first[1], second[1]), axis=1)
    grad_down = jnp.concatenate((first[2].T, second[2].T), axis=0)

    d_in = d_in_bias.reshape(2, 4, half)
    d_in = jnp.where(c == 0, d_in, d_in[::-1]).transpose(1, 0, 2).reshape(4, units)
    small = jnp.concatenate(
        (
            by_index(sum_q[:, 0], t).reshape(-1),
            by_index(sum_kv[:, 0, feat:], t).reshape(-1),
            by_index(d_in, t).reshape(-1),
            sums_one[:3].reshape(-1),
            sums_two[:3].reshape(-1),
        )
    ).reshape(-1, width)
    small = sum_everywhere(small, size)
    q_rows = 4 * feat // width
    at = 2 * q_rows
    d_q = lax.dynamic_slice_in_dim(small[:q_rows].reshape(-1), t * feat, feat, 0)
    d_v = lax.dynamic_slice_in_dim(small[q_rows:at].reshape(-1), t * feat, feat, 0)
    in_rows = 4 * units // width
    d_in_mine = lax.dynamic_slice_in_dim(small[at : at + in_rows].reshape(-1), t * units, units, 0)
    at += in_rows
    return (
        layer_output,
        grad_tokens,
        grad_qkv,
        jnp.stack((d_q, d_v)),
        grad_out,
        small[at + 2],
        grad_in,
        d_in_mine,
        grad_down,
        small[at + 5],
        jnp.stack((small[at], small[at + 3])),
        jnp.stack((small[at + 1], small[at + 4])),
    )


def solution(mesh):
    placed = (
        P("fsdp", "ctx", None),
        P("fsdp"),
        P(None, "fsdp", "tp"),
        P(None, "tp"),
        P("tp", "fsdp"),
        P(),
        P("fsdp", "tp"),
        P("tp"),
        P("tp", "fsdp"),
        P(),
        P(),
        P(),
        P("fsdp", "ctx", None),
    )
    return jax.shard_map(
        per_device,
        mesh=mesh,
        in_specs=placed,
        out_specs=(
            P("fsdp", "ctx", None),
            P("fsdp", "ctx", None),
            P(None, "fsdp", "tp"),
            P(None, "tp"),
            P("tp", "fsdp"),
            P(),
            P("fsdp", "tp"),
            P("tp"),
            P("tp", "fsdp"),
            P(),
            P(),
            P(),
        ),
        check_vma=False,
    )
```

time: 932 us -> 440 us (0.47)
  waiting for transfers between devices: 410 us -> 94 us
  matrix products: 257 us -> 0 us
  Pallas kernels: 0 us -> 143 us
  blocking collectives: 86.9 us -> 0 us
  starting transfers between devices: 1.37 us -> 72.6 us
  other arithmetic: 86.7 us -> 62.4 us
  between operations: 17.3 us -> 1.46 us
    psum x5 -> x0, waiting for transfers between devices: 293 us -> none  [the longest x1 86.1 us: per_device(): lax.psum(attn_part.astype(jnp.bfloat16), 'tp').astype(jnp.float32)]
    dot_general x48 -> x0, matrix products: 257 us -> none  [the longest x4 72.7 us: attend_back(): jnp.einsum('hqk,qhd->khd', grad_scores, queries, preferred_element_type=j...]
    pallas_call x0 -> x7, Pallas kernels: none -> 143 us  [the longest x1 36.8 us: ffn_back_call(): pl.pallas_call(ffn_back_kernel, grid_spec=pltpu.PrefetchScalarGridSpec(nu...]
    ppermute x0 -> x67, waiting for transfers between devices: none -> 94 us  [the longest x5 24.1 us: plane_gather(): from_y = lax.ppermute(mine, 'tp', Y_SWAP)]
    unnamed x23 -> x0, waiting for transfers between devices: 93.8 us -> none
    ppermute x0 -> x67, starting transfers between devices: none -> 72.6 us  [the longest x9 19 us: column_gather(): got = lax.ppermute(shard, 'fsdp', ring(size, step))]
    reduce_sum x20 -> x0, other arithmetic: 46.8 us -> none  [the longest x3 12.6 us: layer_norm(): return centred * lax.rsqrt(spread + epsilon) * gain_row + shift_row]
    all_gather x2 -> x0, blocking collectives: 46.1 us -> none  [the longest x1 31.5 us: fetch_weights(): lax.all_gather(qkv_weight, 'fsdp', axis=1, tiled=True)]
  transfers between devices with their start and end apart: 19 -> 67, of which waited for: 9 -> 25; matrix products, arithmetic and copies ran while one was open for 28% -> 26% of each run, Pallas kernels for 0% -> 7%
where the time goes in v1:
time: 440 us; the launch traced here: 438 us
  Pallas kernels  143 us (32%)
  waiting for transfers between devices  94 us (21%)
  starting transfers between devices  72.6 us (16%)
  local copies, waits for them, and re-layouts  63.7 us (14%)
  other arithmetic  62.4 us (14%)
    pallas_call x1, Pallas kernels, ffn_back_call(): pl.pallas_call(ffn_back_kernel, grid_spec=pltpu.PrefetchScalarGridSpec(nu...  36.8 us
    pallas_call x1, Pallas kernels, ffn_call(): pl.pallas_call(ffn_kernel, grid_spec=pltpu.PrefetchScalarGridSpec(num_sca...  32.2 us
    pallas_call x1, Pallas kernels, attn_back_call(): pl.pallas_call(attn_back_kernel, grid_spec=pltpu.PrefetchScalarGridSpec(n...  27 us
    ppermute x5, waiting for transfers between devices, plane_gather(): from_y = lax.ppermute(mine, 'tp', Y_SWAP)  24.1 us
    another operation x6, other arithmetic, weight_gather(): return jnp.stack((mine, lax.ppermute(mine, 'ctx', C_SWAP)))  23.5 us
    ppermute x3, waiting for transfers between devices, plane_scatter(): got = lax.ppermute(jnp.stack((up[1], up[3])), 'tp', X_SWAP)  23.2 us
    pallas_call x1, Pallas kernels, attn_call(): pl.pallas_call(attn_kernel, grid_spec=pltpu.PrefetchScalarGridSpec(num_sc...  19 us
    ppermute x9, starting transfers between devices, column_gather(): got = lax.ppermute(shard, 'fsdp', ring(size, step))  19 us
  transfers between devices with their start and end apart: 67, of which 25 were waited for; matrix products, arithmetic and copies ran while one was open for 26% of the time, Pallas kernels for 7%

profile of v1, /device:TPU:0, one launch (start us, length us, event | category | flops | bytes accessed | tf_op | source)
XLA Modules:
  0.0 437.6 jit_solution(12382249036247998100)
XLA Ops:
  4.5 3.1 collective-permute-start
  7.6 2.6 collective-permute-start.1
  11.5 3.2 collective-permute-done
  14.7 1.6 constant_dynamic-update-slice_fusion.10
  16.3 3.8 collective-permute-done.1
  21.4 1.5 collective-permute-start.4
  23.0 1.5 collective-permute-start.3
  25.5 3.0 collective-permute-start.20
  28.5 2.3 collective-permute-start.21
  31.9 5.0 %collective-permute-done.4 = bf16[768,384]{1,0:T(8,128)(2,1)} collective-permute-done((bf16[768,384]{1,0:T(8,128)(2,1)}, bf16[768,384]{1,0:T(8,128)(2,1)}, u32[]{:S(2)}, u32[]{:S(2)}) %collective-permute-start.4) | collective-permute-done | bytes 589856 | tf_op jit(solution)/shard_map/ppermute | solution.py:614
  37.9 1.6 collective-permute-start.5
  40.5 1.6 collective-permute-start.6
  43.6 3.0 collective-permute-start.12
  49.3 3.6 fusion.40
  54.1 1.5 collective-permute-start.23
  59.2 10.0 %collective-permute-done.24 = bf16[768,384]{1,0:T(8,128)(2,1)S(1)} collective-permute-done((bf16[768,384]{1,0:T(8,128)(2,1)S(1)}, bf16[768,384]{1,0:T(8,128)(2,1)S(1)}, u32[]{:S(2)}, u32[]{:S(2)}) %collective-permute-start.24) | collective-permute-done | bytes 589856 | tf_op jit(solution)/shard_map/ppermute | solution.py:614
  71.3 1.5 collective-permute-start.26
  72.9 9.1 %collective-permute-done.16 = bf16[768,384]{1,0:T(8,128)(2,1)} collective-permute-done((bf16[768,384]{1,0:T(8,128)(2,1)}, bf16[768,384]{1,0:T(8,128)(2,1)}, u32[]{:S(2)}, u32[]{:S(2)}) %collective-permute-start.16) | collective-permute-done | bytes 589856 | tf_op jit(solution)/shard_map/ppermute | solution.py:614
  85.0 1.6 collective-permute-start.18
  86.6 2.7 collective-permute-done.25
  90.5 2.5 fusion.38
  93.0 1.8 collective-permute-done.17
  94.9 3.6 fusion.39
  98.5 1.6 collective-permute-start.8
  104.8 1.4 collective-permute-done.10
  107.4 5.1 %pad_maximum_fusion.a_ref.wo_ref.wa_ref = bf16[2,4,768,384]{3,2,1,0:T(8,128)(2,1)} fusion(bf16[1,4,768,384]{3,2,1,0:T(8,128)(2,1)} %bitcast.11, bf16[1,4,768,384]{3,2,1,0:T(8,128)(2,1)} %get-tuple-element.118), kind=kLoop, calls=%fused_computation.6 | loop fusion | flops 2359296 | bytes 9437184 | tf_op jit(solution)/shard_map/stack | solution.py:641
  112.5 7.2 %qkv.1 = (bf16[4,512,192]{2,1,0:T(8,128)(2,1)}, bf16[4,512,384]{2,1,0:T(8,128)(2,1)}) custom-call(s32[2]{0:T(128)} %pad_add_fusion.info, bf16[512,768]{1,0:T(8,128)(2,1)} %dynamic-slice_bitcast_fusion.1.x_ref, bf16[2,4,768,384]{3,2,1,0:T(8,128)(2,1)} %pad_maximum_fusion.a_ref.wo_ref.wa_ref, f32[4,1,192]{2,1,0:T(1,128)} %pad_maximum_fusion.18.qb_ref, ...), custom_call_target="tpu_custom_call" | custom-call | flops 1811939328 | bytes 8000000 | tf_op jit(solution)/shard_map/qkv/pallas_call | solution.py:67
  120.4 2.1 dynamic-slice_bitcast_fusion.cot_ref
  123.4 4.5 %pad_maximum_fusion.2 = bf16[2,4,768,384]{3,2,1,0:T(8,128)(2,1)} fusion(bf16[1,4,768,384]{3,2,1,0:T(8,128)(2,1)} %bitcast.30, bf16[1,4,768,384]{3,2,1,0:T(8,128)(2,1)S(1)} %copy-done.2), kind=kLoop, calls=%fused_computation.8 | loop fusion | flops 2359296 | bytes 9437184 | tf_op jit(solution)/shard_map/stack | solution.py:641
  127.9 4.3 pad_maximum_fusion.1
  132.2 19.0 %attn.1 = (bf16[4,512,192]{2,1,0:T(8,128)(2,1)}, f32[4,512,128]{2,1,0:T(8,128)}) custom-call(s32[2]{0:T(128)} %pad_add_fusion.info, bf16[4,512,192]{2,1,0:T(8,128)(2,1)} %get-tuple-element.38.q_ref, bf16[4,512,384]{2,1,0:T(8,128)(2,1)} %get-tuple-element.39.kv_ref, bf16[4,512,384]{2,1,0:T(8,128)(2,1)} %collective-permute-done.11.kvo_ref), custom_call_target="tpu_custom_call" | custom-call | flops 6442450944 | bytes 8000000 | tf_op jit(solution)/shard_map/attn/pallas_call | solution.py:141
  151.1 32.2 %ffn.1 = (bf16[8,512,384]{2,1,0:T(8,128)(2,1)}, f32[8,512,384]{2,1,0:T(8,128)}, bf16[512,768]{1,0:T(8,128)(2,1)}, f32[512,768]{1,0:T(8,128)}, f32[512,128]{1,0:T...) custom-call(s32[2]{0:T(128)} %pad_add_fusion.info, ...), custom_call_target="tpu_custom_call" | custom-call | flops 14495514624 | bytes 30000000 | tf_op jit(solution)/shard_map/ffn/pallas_call | solution.py:325
  183.4 36.8 %ffn_back.1 = (bf16[8,768,384]{2,1,0:T(8,128)(2,1)}, f32[8,1,384]{2,1,0:T(1,128)}, f32[512,768]{1,0:T(8,128)}, bf16[512,768]{1,0:T(8,128)(2,1)}, bf16[4,512,192]...) custom-call(s32[2]{0:T(128)} %pad_add_fusion.info, bf16[512,768]{1,0:T(8,128)(2,1)} %get-tuple-element.43.gb_ref, ...), custom_call_target="tpu_custom_call" | custom-call | flops 7247757312 | bytes 30000000 | tf_op jit(solution)/shard_map/ffn_back/pallas_call | solution.py:470
  220.2 27.0 %attn_back.1 = (bf16[4,512,192]{2,1,0:T(8,128)(2,1)}, f32[4,512,384]{2,1,0:T(8,128)}, bf16[4,512,384]{2,1,0:T(8,128)(2,1)}) custom-call(s32[2]{0:T(128)} %pad_add_fusion.info, bf16[4,512,192]{2,1,0:T(8,128)(2,1)} %get-tuple-element.38.q_ref, bf16[4,512,384]{2,1,0:T(8,128)(2,1)} %get-tuple-element.39.kv_ref, ...), custom_call_target="tpu_custom_call" | custom-call | flops 16106127360 | bytes 12000000 | tf_op jit(solution)/shard_map/attn_back/pallas_call | solution.py:206
  254.3 3.4 slice.298
  257.7 9.7 %down_grad.1 = bf16[8,768,384]{2,1,0:T(8,128)(2,1)} custom-call(s32[2]{0:T(128)} %pad_add_fusion.info, bf16[512,768]{1,0:T(8,128)(2,1)} %get-tuple-element.43.gb_ref, bf16[8,512,384]{2,1,0:T(8,128)(2,1)} %get-tuple-element.58.act_ref), custom_call_target="tpu_custom_call" | custom-call | flops 2415919104 | bytes 9000000 | tf_op jit(solution)/shard_map/down_grad/pallas_call | solution.py:382
  267.4 3.4 slice.386
  274.8 1.8 slice.362
  277.6 11.7 %qkv_back.1 = (bf16[2,4,768,384]{3,2,1,0:T(8,128)(2,1)}, bf16[512,768]{1,0:T(8,128)(2,1)}, f32[4,1,192]{2,1,0:T(1,128)}, f32[4,1,384]{2,1,0:T(1,128)}) custom-call(s32[2]{0:T(128)} %pad_add_fusion.info, bf16[512,768]{1,0:T(8,128)(2,1)} %dynamic-slice_bitcast_fusion.1.x_ref, bf16[4,512,192]{2,1,0:T(8,128)(2,1)} %get-tuple-element.50.gq_ref, ...), custom_call_target="tpu_custom_call" | custom-call | flops 3623878656 | bytes 20000000 | tf_op jit(solution)/shard_map/qkv_back/pallas_call | solution.py:550
  293.2 1.4 slice_reduce_fusion.2
  305.6 1.4 reshape.178
  311.7 1.8 collective-permute-done.63
  317.9 2.1 collective-permute-start.65
  320.1 1.7 slice_bitcast_fusion
  322.1 2.3 collective-permute-start.66
  324.4 3.2 broadcast_in_dim.61
  330.4 3.1 add_convert_fusion.1
  335.9 2.4 add_convert_fusion
  344.4 5.6 %collective-permute-done.46 = bf16[2,384,384]{2,1,0:T(8,128)(2,1)S(1)} collective-permute-done((bf16[2,384,384]{2,1,0:T(8,128)(2,1)S(1)}, bf16[2,384,384]{2,1,0:T(8,128)(2,1)S(1)}, u32[]{:S(2)}, u32[]{:S(2)}) %collective-permute-start.46) | collective-permute-done | bytes 589856 | tf_op jit(solution)/shard_map/ppermute | solution.py:627
  353.3 9.3 %collective-permute-done.54 = bf16[2,384,384]{2,1,0:T(8,128)(2,1)S(1)} collective-permute-done((bf16[2,384,384]{2,1,0:T(8,128)(2,1)S(1)}, bf16[2,384,384]{2,1,0:T(8,128)(2,1)S(1)}, u32[]{:S(2)}, u32[]{:S(2)}) %collective-permute-start.54) | collective-permute-done | bytes 589856 | tf_op jit(solution)/shard_map/ppermute | solution.py:627
  366.0 2.2 fusion
  372.5 3.9 collective-permute-done.55
  377.1 1.9 collective-permute-start.52
  379.2 8.2 %collective-permute-done.38 = bf16[2,384,384]{2,1,0:T(8,128)(2,1)S(1)} collective-permute-done((bf16[2,384,384]{2,1,0:T(8,128)(2,1)S(1)}, bf16[2,384,384]{2,1,0:T(8,128)(2,1)S(1)}, u32[]{:S(2)}, u32[]{:S(2)}) %collective-permute-start.38) | collective-permute-done | bytes 589856 | tf_op jit(solution)/shard_map/ppermute | solution.py:627
  393.9 4.5 %collective-permute-done.39 = bf16[384,384]{1,0:T(8,128)(2,1)S(1)} collective-permute-done((bf16[384,384]{1,0:T(8,128)(2,1)S(1)}, bf16[384,384]{1,0:T(8,128)(2,1)S(1)}, u32[]{:S(2)}, u32[]{:S(2)}) %collective-permute-start.39) | collective-permute-done | bytes 294944 | tf_op jit(solution)/shard_map/ppermute | solution.py:633
  399.3 2.2 collective-permute-start.60
  402.7 9.5 %collective-permute-done.59 = bf16[192,384]{1,0:T(8,128)(2,1)S(1)} collective-permute-done((bf16[192,384]{1,0:T(8,128)(2,1)S(1)}, bf16[192,384]{1,0:T(8,128)(2,1)S(1)}, u32[]{:S(2)}, u32[]{:S(2)}) %collective-permute-start.59) | collective-permute-done | bytes 147488 | tf_op jit(solution)/shard_map/ppermute | solution.py:607
  412.5 7.7 %collective-permute-done.43 = bf16[192,384]{1,0:T(8,128)(2,1)S(1)} collective-permute-done((bf16[192,384]{1,0:T(8,128)(2,1)S(1)}, bf16[192,384]{1,0:T(8,128)(2,1)S(1)}, u32[]{:S(2)}, u32[]{:S(2)}) %collective-permute-start.43) | collective-permute-done | bytes 147488 | tf_op jit(solution)/shard_map/ppermute | solution.py:607
  420.1 1.7 collective-permute-done.44
  422.2 2.4 convert_dynamic-update-slice_fusion.1
  424.6 2.4 convert_dynamic-update-slice_fusion
  431.0 2.0 copy.38
  433.0 2.0 pad_maximum_fusion.11
  434.9 1.8 pad_maximum_fusion.10
  (307 shorter events, 106.9 us)
Async XLA Ops:
  4.5 10.2 %collective-permute-start = (bf16[192,384]{1,0:T(8,128)(2,1)}, bf16[192,384]{1,0:T(8,128)(2,1)}, u32[]{:S(2)}, u32[]{:S(2)}) collective-permute-start(bf16[192,384]{1,0:T(8,128)(2,1)} %get-tuple-element.95), channel_id=1, source_target_pairs={{0,8},{8,16},{16,24},{24,0},{1,9},{9,17},{17,25},{25,1},{2,10},{10... | collective-permute-start | bytes 442376 | tf_op jit(solution)/shard_map/ppermute | solution.py:595
  7.6 12.5 %collective-permute-start.1 = (bf16[192,384]{1,0:T(8,128)(2,1)}, bf16[192,384]{1,0:T(8,128)(2,1)S(1)}, u32[]{:S(2)}, u32[]{:S(2)}) collective-permute-start(bf16[192,384]{1,0:T(8,128)(2,1)} %get-tuple-element.95), channel_id=1, source_target_pairs={{0,16},{8,24},{16,0},{24,8},{1,17},{9,25},{17,1},{25,9},{2,18},{10... | collective-permute-start | bytes 442376 | tf_op jit(solution)/shard_map/ppermute | solution.py:595
  10.2 10.6 %collective-permute-start.2 = (bf16[192,384]{1,0:T(8,128)(2,1)}, bf16[192,384]{1,0:T(8,128)(2,1)S(1)}, u32[]{:S(2)}, u32[]{:S(2)}) collective-permute-start(bf16[192,384]{1,0:T(8,128)(2,1)} %get-tuple-element.95), channel_id=1, source_target_pairs={{0,24},{8,0},{16,8},{24,16},{1,25},{9,1},{17,9},{25,17},{2,26},{10... | collective-permute-start | bytes 442376 | tf_op jit(solution)/shard_map/ppermute | solution.py:595
  21.4 15.5 %collective-permute-start.4 = (bf16[768,384]{1,0:T(8,128)(2,1)}, bf16[768,384]{1,0:T(8,128)(2,1)}, u32[]{:S(2)}, u32[]{:S(2)}) collective-permute-start(bf16[768,384]{1,0:T(8,128)(2,1)} %constant_dynamic-update-slice_fusion.8), channel_id=1, source_target_pairs={{0,2},{2,0},{1,3},{3,1},{4,6},{6,4},{5,7},{7,5},{8,10},{10,8},{9,1... | collective-permute-start | bytes 1769480 | tf_op jit(solution)/shard_map/ppermute | solution.py:614
  23.0 16.5 %collective-permute-start.3 = (bf16[768,384]{1,0:T(8,128)(2,1)}, bf16[768,384]{1,0:T(8,128)(2,1)}, u32[]{:S(2)}, u32[]{:S(2)}) collective-permute-start(bf16[768,384]{1,0:T(8,128)(2,1)} %constant_dynamic-update-slice_fusion.8), channel_id=1, source_target_pairs={{0,1},{1,0},{2,3},{3,2},{4,5},{5,4},{6,7},{7,6},{8,9},{9,8},{10,11... | collective-permute-start | bytes 1769480 | tf_op jit(solution)/shard_map/ppermute | solution.py:613
  25.5 18.1 %collective-permute-start.20 = (bf16[192,384]{1,0:T(8,128)(2,1)S(1)}, bf16[192,384]{1,0:T(8,128)(2,1)S(1)}, u32[]{:S(2)}, u32[]{:S(2)}) collective-permute-start(bf16[192,384]{1,0:T(8,128)(2,1)S(1)} %get-tuple-element.91), channel_id=1, source_target_pairs={{0,8},{8,16},{16,24},{24,0},{1,9},{9,17},{17,25},{25,1},{2,10},{10... | collective-permute-start | bytes 442376 | tf_op jit(solution)/shard_map/ppermute | solution.py:595
  28.5 18.2 %collective-permute-start.21 = (bf16[192,384]{1,0:T(8,128)(2,1)S(1)}, bf16[192,384]{1,0:T(8,128)(2,1)S(1)}, u32[]{:S(2)}, u32[]{:S(2)}) collective-permute-start(bf16[192,384]{1,0:T(8,128)(2,1)S(1)} %get-tuple-element.91), channel_id=1, source_target_pairs={{0,16},{8,24},{16,0},{24,8},{1,17},{9,25},{17,1},{25,9},{2,18},{10... | collective-permute-start | bytes 442376 | tf_op jit(solution)/shard_map/ppermute | solution.py:595
  30.8 22.1 %collective-permute-start.22 = (bf16[192,384]{1,0:T(8,128)(2,1)S(1)}, bf16[192,384]{1,0:T(8,128)(2,1)S(1)}, u32[]{:S(2)}, u32[]{:S(2)}) collective-permute-start(bf16[192,384]{1,0:T(8,128)(2,1)S(1)} %get-tuple-element.91), channel_id=1, source_target_pairs={{0,24},{8,0},{16,8},{24,16},{1,25},{9,1},{17,9},{25,17},{2,26},{10... | collective-permute-start | bytes 442376 | tf_op jit(solution)/shard_map/ppermute | solution.py:595
  37.9 10.2 %collective-permute-start.5 = (bf16[384,384]{1,0:T(8,128)(2,1)S(1)}, bf16[384,384]{1,0:T(8,128)(2,1)S(1)}, u32[]{:S(2)}, u32[]{:S(2)}) collective-permute-start(bf16[384,384]{1,0:T(8,128)(2,1)S(1)} %slice.355), channel_id=1, source_target_pairs={{0,1},{1,0},{2,3},{3,2},{4,5},{5,4},{6,7},{7,6},{8,9},{9,8},{10,11... | collective-permute-start | bytes 884744 | tf_op jit(solution)/shard_map/ppermute | solution.py:615
  40.5 8.8 %collective-permute-start.6 = (bf16[384,384]{1,0:T(8,128)(2,1)S(1)}, bf16[384,384]{1,0:T(8,128)(2,1)S(1)}, u32[]{:S(2)}, u32[]{:S(2)}) collective-permute-start(bf16[384,384]{1,0:T(8,128)(2,1)S(1)} %slice.356), channel_id=1, source_target_pairs={{0,2},{2,0},{1,3},{3,1},{4,6},{6,4},{5,7},{7,5},{8,10},{10,8},{9,1... | collective-permute-start | bytes 884744 | tf_op jit(solution)/shard_map/ppermute | solution.py:616
  43.6 10.5 %collective-permute-start.12 = (bf16[192,384]{1,0:T(8,128)(2,1)S(1)}, bf16[192,384]{1,0:T(8,128)(2,1)S(1)}, u32[]{:S(2)}, u32[]{:S(2)}) collective-permute-start(bf16[192,384]{1,0:T(8,128)(2,1)S(1)} %get-tuple-element.93), channel_id=1, source_target_pairs={{0,8},{8,16},{16,24},{24,0},{1,9},{9,17},{17,25},{25,1},{2,10},{10... | collective-permute-start | bytes 442376 | tf_op jit(solution)/shard_map/ppermute | solution.py:595
  46.7 9.7 %collective-permute-start.13 = (bf16[192,384]{1,0:T(8,128)(2,1)S(1)}, bf16[192,384]{1,0:T(8,128)(2,1)S(1)}, u32[]{:S(2)}, u32[]{:S(2)}) collective-permute-start(bf16[192,384]{1,0:T(8,128)(2,1)S(1)} %get-tuple-element.93), channel_id=1, source_target_pairs={{0,16},{8,24},{16,0},{24,8},{1,17},{9,25},{17,1},{25,9},{2,18},{10... | collective-permute-start | bytes 442376 | tf_op jit(solution)/shard_map/ppermute | solution.py:595
  48.1 9.0 %collective-permute-start.14 = (bf16[192,384]{1,0:T(8,128)(2,1)S(1)}, bf16[192,384]{1,0:T(8,128)(2,1)S(1)}, u32[]{:S(2)}, u32[]{:S(2)}) collective-permute-start(bf16[192,384]{1,0:T(8,128)(2,1)S(1)} %get-tuple-element.93), channel_id=1, source_target_pairs={{0,24},{8,0},{16,8},{24,16},{1,25},{9,1},{17,9},{25,17},{2,26},{10... | collective-permute-start | bytes 442376 | tf_op jit(solution)/shard_map/ppermute | solution.py:595
  52.9 54.5 %collective-permute-start.7 = (bf16[4,768,384]{2,1,0:T(8,128)(2,1)}, bf16[4,768,384]{2,1,0:T(8,128)(2,1)}, u32[]{:S(2)}, u32[]{:S(2)}) collective-permute-start(bf16[4,768,384]{2,1,0:T(8,128)(2,1)} %get-tuple-element.119), channel_id=1, source_target_pairs={{0,4},{4,0},{1,5},{5,1},{2,6},{6,2},{3,7},{7,3},{8,12},{12,8},{9,1... | collective-permute-start | bytes 7077896 | tf_op jit(solution)/shard_map/ppermute | solution.py:641
  52.9 16.3 %collective-permute-start.24 = (bf16[768,384]{1,0:T(8,128)(2,1)S(1)}, bf16[768,384]{1,0:T(8,128)(2,1)S(1)}, u32[]{:S(2)}, u32[]{:S(2)}) collective-permute-start(bf16[768,384]{1,0:T(8,128)(2,1)S(1)} %constant_dynamic-update-slice_fusion), channel_id=1, source_target_pairs={{0,2},{2,0},{1,3},{3,1},{4,6},{6,4},{5,7},{7,5},{8,10},{10,8},{9,1... | collective-permute-start | bytes 1769480 | tf_op jit(solution)/shard_map/ppermute | solution.py:614
  54.1 16.3 %collective-permute-start.23 = (bf16[768,384]{1,0:T(8,128)(2,1)S(1)}, bf16[768,384]{1,0:T(8,128)(2,1)S(1)}, u32[]{:S(2)}, u32[]{:S(2)}) collective-permute-start(bf16[768,384]{1,0:T(8,128)(2,1)S(1)} %constant_dynamic-update-slice_fusion), channel_id=1, source_target_pairs={{0,1},{1,0},{2,3},{3,2},{4,5},{5,4},{6,7},{7,6},{8,9},{9,8},{10,11... | collective-permute-start | bytes 1769480 | tf_op jit(solution)/shard_map/ppermute | solution.py:613
  57.8 24.1 %collective-permute-start.16 = (bf16[768,384]{1,0:T(8,128)(2,1)}, bf16[768,384]{1,0:T(8,128)(2,1)}, u32[]{:S(2)}, u32[]{:S(2)}) collective-permute-start(bf16[768,384]{1,0:T(8,128)(2,1)} %constant_dynamic-update-slice_fusion.4), channel_id=1, source_target_pairs={{0,2},{2,0},{1,3},{3,1},{4,6},{6,4},{5,7},{7,5},{8,10},{10,8},{9,1... | collective-permute-start | bytes 1769480 | tf_op jit(solution)/shard_map/ppermute | solution.py:614
  58.3 25.7 %collective-permute-start.15 = (bf16[768,384]{1,0:T(8,128)(2,1)}, bf16[768,384]{1,0:T(8,128)(2,1)}, u32[]{:S(2)}, u32[]{:S(2)}) collective-permute-start(bf16[768,384]{1,0:T(8,128)(2,1)} %constant_dynamic-update-slice_fusion.4), channel_id=1, source_target_pairs={{0,1},{1,0},{2,3},{3,2},{4,5},{5,4},{6,7},{7,6},{8,9},{9,8},{10,11... | collective-permute-start | bytes 1769480 | tf_op jit(solution)/shard_map/ppermute | solution.py:613
  69.2 20.1 %collective-permute-start.25 = (bf16[384,384]{1,0:T(8,128)(2,1)S(1)}, bf16[384,384]{1,0:T(8,128)(2,1)}, u32[]{:S(2)}, u32[]{:S(2)}) collective-permute-start(bf16[384,384]{1,0:T(8,128)(2,1)S(1)} %slice.359), channel_id=1, source_target_pairs={{0,1},{1,0},{2,3},{3,2},{4,5},{5,4},{6,7},{7,6},{8,9},{9,8},{10,11... | collective-permute-start | bytes 884744 | tf_op jit(solution)/shard_map/ppermute | solution.py:615
  71.3 18.1 %collective-permute-start.26 = (bf16[384,384]{1,0:T(8,128)(2,1)}, bf16[384,384]{1,0:T(8,128)(2,1)}, u32[]{:S(2)}, u32[]{:S(2)}) collective-permute-start(bf16[384,384]{1,0:T(8,128)(2,1)} %slice.360), channel_id=1, source_target_pairs={{0,2},{2,0},{1,3},{3,1},{4,6},{6,4},{5,7},{7,5},{8,10},{10,8},{9,1... | collective-permute-start | bytes 884744 | tf_op jit(solution)/shard_map/ppermute | solution.py:616
  82.9 11.9 %collective-permute-start.17 = (bf16[384,384]{1,0:T(8,128)(2,1)S(1)}, bf16[384,384]{1,0:T(8,128)(2,1)S(1)}, u32[]{:S(2)}, u32[]{:S(2)}) collective-permute-start(bf16[384,384]{1,0:T(8,128)(2,1)S(1)} %slice.357), channel_id=1, source_target_pairs={{0,1},{1,0},{2,3},{3,2},{4,5},{5,4},{6,7},{7,6},{8,9},{9,8},{10,11... | collective-permute-start | bytes 884744 | tf_op jit(solution)/shard_map/ppermute | solution.py:615
  85.0 9.8 %collective-permute-start.18 = (bf16[384,384]{1,0:T(8,128)(2,1)S(1)}, bf16[384,384]{1,0:T(8,128)(2,1)S(1)}, u32[]{:S(2)}, u32[]{:S(2)}) collective-permute-start(bf16[384,384]{1,0:T(8,128)(2,1)S(1)} %slice.358), channel_id=1, source_target_pairs={{0,2},{2,0},{1,3},{3,1},{4,6},{6,4},{5,7},{7,5},{8,10},{10,8},{9,1... | collective-permute-start | bytes 884744 | tf_op jit(solution)/shard_map/ppermute | solution.py:616
  93.0 30.4 %collective-permute-start.27 = (bf16[4,768,384]{2,1,0:T(8,128)(2,1)}, bf16[4,768,384]{2,1,0:T(8,128)(2,1)}, u32[]{:S(2)}, u32[]{:S(2)}) collective-permute-start(bf16[4,768,384]{2,1,0:T(8,128)(2,1)} %get-tuple-element.115), channel_id=1, source_target_pairs={{0,4},{4,0},{1,5},{5,1},{2,6},{6,2},{3,7},{7,3},{8,12},{12,8},{9,1... | collective-permute-start | bytes 7077896 | tf_op jit(solution)/shard_map/ppermute | solution.py:641
  98.5 29.4 %collective-permute-start.19 = (bf16[4,768,384]{2,1,0:T(8,128)(2,1)}, bf16[4,768,384]{2,1,0:T(8,128)(2,1)}, u32[]{:S(2)}, u32[]{:S(2)}) collective-permute-start(bf16[4,768,384]{2,1,0:T(8,128)(2,1)} %get-tuple-element.117), channel_id=1, source_target_pairs={{0,4},{4,0},{1,5},{5,1},{2,6},{6,2},{3,7},{7,3},{8,12},{12,8},{9,1... | collective-permute-start | bytes 7077896 | tf_op jit(solution)/shard_map/ppermute | solution.py:641
  100.1 4.8 %collective-permute-start.9 = (f32[1,1152]{1,0:T(1,128)S(1)}, f32[1,1152]{1,0:T(1,128)S(1)}, u32[]{:S(2)}, u32[]{:S(2)}) collective-permute-start(f32[1,1152]{1,0:T(1,128)S(1)} %reshape.169), channel_id=1, source_target_pairs={{0,2},{2,0},{1,3},{3,1},{4,6},{6,4},{5,7},{7,5},{8,10},{10,8},{9,1... | collective-permute-start | bytes 13832 | tf_op jit(solution)/shard_map/ppermute | solution.py:701
  119.7 12.5 %collective-permute-start.11 = (bf16[4,512,384]{2,1,0:T(8,128)(2,1)}, bf16[4,512,384]{2,1,0:T(8,128)(2,1)}, u32[]{:S(2)}, u32[]{:S(2)}) collective-permute-start(bf16[4,512,384]{2,1,0:T(8,128)(2,1)} %get-tuple-element.39.kv_ref), channel_id=1, source_target_pairs={{0,4},{4,0},{1,5},{5,1},{2,6},{6,2},{3,7},{7,3},{8,12},{12,8},{9,1... | collective-permute-start | bytes 4718600 | tf_op jit(solution)/shard_map/ppermute | solution.py:716
  247.2 30.4 %collective-permute-start.32 = (bf16[4,512,384]{2,1,0:T(8,128)(2,1)}, bf16[4,512,384]{2,1,0:T(8,128)(2,1)}, u32[]{:S(2)}, u32[]{:S(2)}) collective-permute-start(bf16[4,512,384]{2,1,0:T(8,128)(2,1)} %get-tuple-element.52), channel_id=1, source_target_pairs={{0,4},{4,0},{1,5},{5,1},{2,6},{6,2},{3,7},{7,3},{8,12},{12,8},{9,1... | collective-permute-start | bytes 4718600 | tf_op jit(solution)/shard_map/ppermute | solution.py:729
  247.7 27.0 %collective-permute-start.28 = (bf16[512,768]{1,0:T(8,128)(2,1)}, bf16[512,768]{1,0:T(8,128)(2,1)}, u32[]{:S(2)}, u32[]{:S(2)}) collective-permute-start(bf16[512,768]{1,0:T(8,128)(2,1)} %get-tuple-element.41), channel_id=1, source_target_pairs={{0,1},{1,0},{2,3},{3,2},{4,5},{5,4},{6,7},{7,6},{8,9},{9,8},{10,11... | collective-permute-start | bytes 2359304 | tf_op jit(solution)/shard_map/ppermute | solution.py:613
  248.9 23.8 %collective-permute-start.29 = (bf16[512,768]{1,0:T(8,128)(2,1)}, bf16[512,768]{1,0:T(8,128)(2,1)}, u32[]{:S(2)}, u32[]{:S(2)}) collective-permute-start(bf16[512,768]{1,0:T(8,128)(2,1)} %get-tuple-element.41), channel_id=1, source_target_pairs={{0,2},{2,0},{1,3},{3,1},{4,6},{6,4},{5,7},{7,5},{8,10},{10,8},{9,1... | collective-permute-start | bytes 2359304 | tf_op jit(solution)/shard_map/ppermute | solution.py:614
  257.7 72.7 %collective-permute-start.45 = (bf16[4,768,384]{2,1,0:T(8,128)(2,1)}, bf16[4,768,384]{2,1,0:T(8,128)(2,1)}, u32[]{:S(2)}, u32[]{:S(2)}) collective-permute-start(bf16[4,768,384]{2,1,0:T(8,128)(2,1)} %slice.298), channel_id=1, source_target_pairs={{0,4},{4,0},{1,5},{5,1},{2,6},{6,2},{3,7},{7,3},{8,12},{12,8},{9,1... | collective-permute-start | bytes 7077896 | tf_op jit(solution)/shard_map/ppermute | solution.py:645
  270.8 64.1 %collective-permute-start.53 = (bf16[4,768,384]{2,1,0:T(8,128)(2,1)}, bf16[4,768,384]{2,1,0:T(8,128)(2,1)}, u32[]{:S(2)}, u32[]{:S(2)}) collective-permute-start(bf16[4,768,384]{2,1,0:T(8,128)(2,1)} %slice.386), channel_id=1, source_target_pairs={{0,4},{4,0},{1,5},{5,1},{2,6},{6,2},{3,7},{7,3},{8,12},{12,8},{9,1... | collective-permute-start | bytes 7077896 | tf_op jit(solution)/shard_map/ppermute | solution.py:645
  273.8 40.8 %collective-permute-start.30 = (bf16[256,768]{1,0:T(8,128)(2,1)S(1)}, bf16[256,768]{1,0:T(8,128)(2,1)}, u32[]{:S(2)}, u32[]{:S(2)}) collective-permute-start(bf16[256,768]{1,0:T(8,128)(2,1)S(1)} %slice.361), channel_id=1, source_target_pairs={{0,1},{1,0},{2,3},{3,2},{4,5},{5,4},{6,7},{7,6},{8,9},{9,8},{10,11... | collective-permute-start | bytes 1179656 | tf_op jit(solution)/shard_map/ppermute | solution.py:615
  276.5 38.1 %collective-permute-start.31 = (bf16[256,768]{1,0:T(8,128)(2,1)}, bf16[256,768]{1,0:T(8,128)(2,1)}, u32[]{:S(2)}, u32[]{:S(2)}) collective-permute-start(bf16[256,768]{1,0:T(8,128)(2,1)} %slice.362), channel_id=1, source_target_pairs={{0,2},{2,0},{1,3},{3,1},{4,6},{6,4},{5,7},{7,5},{8,10},{10,8},{9,1... | collective-permute-start | bytes 1179656 | tf_op jit(solution)/shard_map/ppermute | solution.py:616
  309.4 4.1 collective-permute-start.63
  313.5 4.4 %collective-permute-start.64 = (f32[12,768]{1,0:T(8,128)S(1)}, f32[12,768]{1,0:T(8,128)S(1)}, u32[]{:S(2)}, u32[]{:S(2)}) collective-permute-start(f32[12,768]{1,0:T(8,128)S(1)} %add.321), channel_id=1, source_target_pairs={{0,2},{2,0},{1,3},{3,1},{4,6},{6,4},{5,7},{7,5},{8,10},{10,8},{9,1... | collective-permute-start | bytes 110600 | tf_op jit(solution)/shard_map/ppermute | solution.py:657
  315.8 22.7 %collective-permute-start.33 = (bf16[512,768]{1,0:T(8,128)(2,1)}, bf16[512,768]{1,0:T(8,128)(2,1)}, u32[]{:S(2)}, u32[]{:S(2)}) collective-permute-start(bf16[512,768]{1,0:T(8,128)(2,1)} %get-tuple-element.55), channel_id=1, source_target_pairs={{0,1},{1,0},{2,3},{3,2},{4,5},{5,4},{6,7},{7,6},{8,9},{9,8},{10,11... | collective-permute-start | bytes 2359304 | tf_op jit(solution)/shard_map/ppermute | solution.py:613
  316.9 22.7 %collective-permute-start.34 = (bf16[512,768]{1,0:T(8,128)(2,1)}, bf16[512,768]{1,0:T(8,128)(2,1)}, u32[]{:S(2)}, u32[]{:S(2)}) collective-permute-start(bf16[512,768]{1,0:T(8,128)(2,1)} %get-tuple-element.55), channel_id=1, source_target_pairs={{0,2},{2,0},{1,3},{3,1},{4,6},{6,4},{5,7},{7,5},{8,10},{10,8},{9,1... | collective-permute-start | bytes 2359304 | tf_op jit(solution)/shard_map/ppermute | solution.py:614
  317.9 4.2 collective-permute-start.65
  322.1 6.8 %collective-permute-start.66 = (f32[12,768]{1,0:T(8,128)S(1)}, f32[12,768]{1,0:T(8,128)S(1)}, u32[]{:S(2)}, u32[]{:S(2)}) collective-permute-start(f32[12,768]{1,0:T(8,128)S(1)} %add.323), channel_id=1, source_target_pairs={{0,16},{8,24},{16,0},{24,8},{1,17},{9,25},{17,1},{25,9},{2,18},{10... | collective-permute-start | bytes 110600 | tf_op jit(solution)/shard_map/ppermute | solution.py:660
  328.9 37.0 %collective-permute-start.37 = (bf16[4,768,384]{2,1,0:T(8,128)(2,1)}, bf16[4,768,384]{2,1,0:T(8,128)(2,1)}, u32[]{:S(2)}, u32[]{:S(2)}) collective-permute-start(bf16[4,768,384]{2,1,0:T(8,128)(2,1)} %slice_bitcast_fusion), channel_id=1, source_target_pairs={{0,4},{4,0},{1,5},{5,1},{2,6},{6,2},{3,7},{7,3},{8,12},{12,8},{9,1... | collective-permute-start | bytes 7077896 | tf_op jit(solution)/shard_map/ppermute | solution.py:645
  333.8 16.3 %collective-permute-start.46 = (bf16[2,384,384]{2,1,0:T(8,128)(2,1)S(1)}, bf16[2,384,384]{2,1,0:T(8,128)(2,1)S(1)}, u32[]{:S(2)}, u32[]{:S(2)}) collective-permute-start(bf16[2,384,384]{2,1,0:T(8,128)(2,1)S(1)} %pad_maximum_fusion.7), channel_id=1, source_target_pairs={{0,1},{1,0},{2,3},{3,2},{4,5},{5,4},{6,7},{7,6},{8,9},{9,8},{10,11... | collective-permute-start | bytes 1769480 | tf_op jit(solution)/shard_map/ppermute | solution.py:627
  334.9 16.2 %collective-permute-start.48 = (bf16[2,384,384]{2,1,0:T(8,128)(2,1)S(1)}, bf16[2,384,384]{2,1,0:T(8,128)(2,1)S(1)}, u32[]{:S(2)}, u32[]{:S(2)}) collective-permute-start(bf16[2,384,384]{2,1,0:T(8,128)(2,1)S(1)} %stack.208), channel_id=1, source_target_pairs={{0,2},{2,0},{1,3},{3,1},{4,6},{6,4},{5,7},{7,5},{8,10},{10,8},{9,1... | collective-permute-start | bytes 1769480 | tf_op jit(solution)/shard_map/ppermute | solution.py:630
  338.5 24.2 %collective-permute-start.54 = (bf16[2,384,384]{2,1,0:T(8,128)(2,1)S(1)}, bf16[2,384,384]{2,1,0:T(8,128)(2,1)S(1)}, u32[]{:S(2)}, u32[]{:S(2)}) collective-permute-start(bf16[2,384,384]{2,1,0:T(8,128)(2,1)S(1)} %pad_maximum_fusion.8), channel_id=1, source_target_pairs={{0,1},{1,0},{2,3},{3,2},{4,5},{5,4},{6,7},{7,6},{8,9},{9,8},{10,11... | collective-permute-start | bytes 1769480 | tf_op jit(solution)/shard_map/ppermute | solution.py:627
  339.6 24.2 %collective-permute-start.56 = (bf16[2,384,384]{2,1,0:T(8,128)(2,1)S(1)}, bf16[2,384,384]{2,1,0:T(8,128)(2,1)S(1)}, u32[]{:S(2)}, u32[]{:S(2)}) collective-permute-start(bf16[2,384,384]{2,1,0:T(8,128)(2,1)S(1)} %stack.209), channel_id=1, source_target_pairs={{0,2},{2,0},{1,3},{3,1},{4,6},{6,4},{5,7},{7,5},{8,10},{10,8},{9,1... | collective-permute-start | bytes 1769480 | tf_op jit(solution)/shard_map/ppermute | solution.py:630
  351.3 18.8 %collective-permute-start.47 = (bf16[384,384]{1,0:T(8,128)(2,1)S(1)}, bf16[384,384]{1,0:T(8,128)(2,1)S(1)}, u32[]{:S(2)}, u32[]{:S(2)}) collective-permute-start(bf16[384,384]{1,0:T(8,128)(2,1)S(1)} %get-tuple-element.105), channel_id=1, source_target_pairs={{0,2},{2,0},{1,3},{3,1},{4,6},{6,4},{5,7},{7,5},{8,10},{10,8},{9,1... | collective-permute-start | bytes 884744 | tf_op jit(solution)/shard_map/ppermute | solution.py:633
  352.3 18.7 %collective-permute-start.49 = (bf16[384,384]{1,0:T(8,128)(2,1)S(1)}, bf16[384,384]{1,0:T(8,128)(2,1)S(1)}, u32[]{:S(2)}, u32[]{:S(2)}) collective-permute-start(bf16[384,384]{1,0:T(8,128)(2,1)S(1)} %get-tuple-element.104), channel_id=1, source_target_pairs={{0,1},{1,0},{2,3},{3,2},{4,5},{5,4},{6,7},{7,6},{8,9},{9,8},{10,11... | collective-permute-start | bytes 884744 | tf_op jit(solution)/shard_map/ppermute | solution.py:634
  363.9 12.5 %collective-permute-start.55 = (bf16[384,384]{1,0:T(8,128)(2,1)S(1)}, bf16[384,384]{1,0:T(8,128)(2,1)S(1)}, u32[]{:S(2)}, u32[]{:S(2)}) collective-permute-start(bf16[384,384]{1,0:T(8,128)(2,1)S(1)} %get-tuple-element.111), channel_id=1, source_target_pairs={{0,2},{2,0},{1,3},{3,1},{4,6},{6,4},{5,7},{7,5},{8,10},{10,8},{9,1... | collective-permute-start | bytes 884744 | tf_op jit(solution)/shard_map/ppermute | solution.py:633
  364.9 12.1 %collective-permute-start.57 = (bf16[384,384]{1,0:T(8,128)(2,1)S(1)}, bf16[384,384]{1,0:T(8,128)(2,1)S(1)}, u32[]{:S(2)}, u32[]{:S(2)}) collective-permute-start(bf16[384,384]{1,0:T(8,128)(2,1)S(1)} %get-tuple-element.110), channel_id=1, source_target_pairs={{0,1},{1,0},{2,3},{3,2},{4,5},{5,4},{6,7},{7,6},{8,9},{9,8},{10,11... | collective-permute-start | bytes 884744 | tf_op jit(solution)/shard_map/ppermute | solution.py:634
  368.5 19.0 %collective-permute-start.38 = (bf16[2,384,384]{2,1,0:T(8,128)(2,1)S(1)}, bf16[2,384,384]{2,1,0:T(8,128)(2,1)S(1)}, u32[]{:S(2)}, u32[]{:S(2)}) collective-permute-start(bf16[2,384,384]{2,1,0:T(8,128)(2,1)S(1)} %pad_maximum_fusion.6), channel_id=1, source_target_pairs={{0,1},{1,0},{2,3},{3,2},{4,5},{5,4},{6,7},{7,6},{8,9},{9,8},{10,11... | collective-permute-start | bytes 1769480 | tf_op jit(solution)/shard_map/ppermute | solution.py:627
  370.1 18.2 %collective-permute-start.40 = (bf16[2,384,384]{2,1,0:T(8,128)(2,1)S(1)}, bf16[2,384,384]{2,1,0:T(8,128)(2,1)S(1)}, u32[]{:S(2)}, u32[]{:S(2)}) collective-permute-start(bf16[2,384,384]{2,1,0:T(8,128)(2,1)S(1)} %stack.207), channel_id=1, source_target_pairs={{0,2},{2,0},{1,3},{3,1},{4,6},{6,4},{5,7},{7,5},{8,10},{10,8},{9,1... | collective-permute-start | bytes 1769480 | tf_op jit(solution)/shard_map/ppermute | solution.py:630
  372.1 19.2 %collective-permute-start.50 = (bf16[192,384]{1,0:T(8,128)(2,1)S(1)}, bf16[192,384]{1,0:T(8,128)(2,1)S(1)}, u32[]{:S(2)}, u32[]{:S(2)}) collective-permute-start(bf16[192,384]{1,0:T(8,128)(2,1)S(1)} %get-tuple-element.131), channel_id=1, source_target_pairs={{0,8},{8,16},{16,24},{24,0},{1,9},{9,17},{17,25},{25,1},{2,10},{10... | collective-permute-start | bytes 442376 | tf_op jit(solution)/shard_map/ppermute | solution.py:607
  376.4 16.0 %collective-permute-start.51 = (bf16[192,384]{1,0:T(8,128)(2,1)S(1)}, bf16[192,384]{1,0:T(8,128)(2,1)S(1)}, u32[]{:S(2)}, u32[]{:S(2)}) collective-permute-start(bf16[192,384]{1,0:T(8,128)(2,1)S(1)} %get-tuple-element.132), channel_id=1, source_target_pairs={{0,16},{8,24},{16,0},{24,8},{1,17},{9,25},{17,1},{25,9},{2,18},{10... | collective-permute-start | bytes 442376 | tf_op jit(solution)/shard_map/ppermute | solution.py:607
  377.1 16.4 %collective-permute-start.52 = (bf16[192,384]{1,0:T(8,128)(2,1)S(1)}, bf16[192,384]{1,0:T(8,128)(2,1)S(1)}, u32[]{:S(2)}, u32[]{:S(2)}) collective-permute-start(bf16[192,384]{1,0:T(8,128)(2,1)S(1)} %get-tuple-element.133), channel_id=1, source_target_pairs={{0,24},{8,0},{16,8},{24,16},{1,25},{9,1},{17,9},{25,17},{2,26},{10... | collective-permute-start | bytes 442376 | tf_op jit(solution)/shard_map/ppermute | solution.py:607
  388.5 9.9 %collective-permute-start.39 = (bf16[384,384]{1,0:T(8,128)(2,1)S(1)}, bf16[384,384]{1,0:T(8,128)(2,1)S(1)}, u32[]{:S(2)}, u32[]{:S(2)}) collective-permute-start(bf16[384,384]{1,0:T(8,128)(2,1)S(1)} %get-tuple-element.99), channel_id=1, source_target_pairs={{0,2},{2,0},{1,3},{3,1},{4,6},{6,4},{5,7},{7,5},{8,10},{10,8},{9,1... | collective-permute-start | bytes 884744 | tf_op jit(solution)/shard_map/ppermute | solution.py:633
  389.5 9.9 %collective-permute-start.41 = (bf16[384,384]{1,0:T(8,128)(2,1)S(1)}, bf16[384,384]{1,0:T(8,128)(2,1)S(1)}, u32[]{:S(2)}, u32[]{:S(2)}) collective-permute-start(bf16[384,384]{1,0:T(8,128)(2,1)S(1)} %get-tuple-element.98), channel_id=1, source_target_pairs={{0,1},{1,0},{2,3},{3,2},{4,5},{5,4},{6,7},{7,6},{8,9},{9,8},{10,11... | collective-permute-start | bytes 884744 | tf_op jit(solution)/shard_map/ppermute | solution.py:634
  391.3 35.7 %collective-permute-start.35 = (bf16[256,768]{1,0:T(8,128)(2,1)S(1)}, bf16[256,768]{1,0:T(8,128)(2,1)S(1)}, u32[]{:S(2)}, u32[]{:S(2)}) collective-permute-start(bf16[256,768]{1,0:T(8,128)(2,1)S(1)} %slice.363), channel_id=1, source_target_pairs={{0,1},{1,0},{2,3},{3,2},{4,5},{5,4},{6,7},{7,6},{8,9},{9,8},{10,11... | collective-permute-start | bytes 1179656 | tf_op jit(solution)/shard_map/ppermute | solution.py:615
  392.4 34.6 %collective-permute-start.36 = (bf16[256,768]{1,0:T(8,128)(2,1)S(1)}, bf16[256,768]{1,0:T(8,128)(2,1)S(1)}, u32[]{:S(2)}, u32[]{:S(2)}) collective-permute-start(bf16[256,768]{1,0:T(8,128)(2,1)S(1)} %slice.364), channel_id=1, source_target_pairs={{0,2},{2,0},{1,3},{3,1},{4,6},{6,4},{5,7},{7,5},{8,10},{10,8},{9,1... | collective-permute-start | bytes 1179656 | tf_op jit(solution)/shard_map/ppermute | solution.py:616
  393.5 9.1 %collective-permute-start.58 = (bf16[192,384]{1,0:T(8,128)(2,1)S(1)}, bf16[192,384]{1,0:T(8,128)(2,1)S(1)}, u32[]{:S(2)}, u32[]{:S(2)}) collective-permute-start(bf16[192,384]{1,0:T(8,128)(2,1)S(1)} %get-tuple-element.134), channel_id=1, source_target_pairs={{0,8},{8,16},{16,24},{24,0},{1,9},{9,17},{17,25},{25,1},{2,10},{10... | collective-permute-start | bytes 442376 | tf_op jit(solution)/shard_map/ppermute | solution.py:607
  398.4 13.8 %collective-permute-start.59 = (bf16[192,384]{1,0:T(8,128)(2,1)S(1)}, bf16[192,384]{1,0:T(8,128)(2,1)S(1)}, u32[]{:S(2)}, u32[]{:S(2)}) collective-permute-start(bf16[192,384]{1,0:T(8,128)(2,1)S(1)} %get-tuple-element.135), channel_id=1, source_target_pairs={{0,16},{8,24},{16,0},{24,8},{1,17},{9,25},{17,1},{25,9},{2,18},{10... | collective-permute-start | bytes 442376 | tf_op jit(solution)/shard_map/ppermute | solution.py:607
  399.3 12.9 %collective-permute-start.60 = (bf16[192,384]{1,0:T(8,128)(2,1)S(1)}, bf16[192,384]{1,0:T(8,128)(2,1)S(1)}, u32[]{:S(2)}, u32[]{:S(2)}) collective-permute-start(bf16[192,384]{1,0:T(8,128)(2,1)S(1)} %get-tuple-element.136), channel_id=1, source_target_pairs={{0,24},{8,0},{16,8},{24,16},{1,25},{9,1},{17,9},{25,17},{2,26},{10... | collective-permute-start | bytes 442376 | tf_op jit(solution)/shard_map/ppermute | solution.py:607
  402.6 9.8 %collective-permute-start.42 = (bf16[192,384]{1,0:T(8,128)(2,1)S(1)}, bf16[192,384]{1,0:T(8,128)(2,1)S(1)}, u32[]{:S(2)}, u32[]{:S(2)}) collective-permute-start(bf16[192,384]{1,0:T(8,128)(2,1)S(1)} %get-tuple-element.128), channel_id=1, source_target_pairs={{0,8},{8,16},{16,24},{24,0},{1,9},{9,17},{17,25},{25,1},{2,10},{10... | collective-permute-start | bytes 442376 | tf_op jit(solution)/shard_map/ppermute | solution.py:607
  412.2 7.9 %collective-permute-start.43 = (bf16[192,384]{1,0:T(8,128)(2,1)S(1)}, bf16[192,384]{1,0:T(8,128)(2,1)S(1)}, u32[]{:S(2)}, u32[]{:S(2)}) collective-permute-start(bf16[192,384]{1,0:T(8,128)(2,1)S(1)} %get-tuple-element.129), channel_id=1, source_target_pairs={{0,16},{8,24},{16,0},{24,8},{1,17},{9,25},{17,1},{25,9},{2,18},{10... | collective-permute-start | bytes 442376 | tf_op jit(solution)/shard_map/ppermute | solution.py:607
  412.2 9.7 %collective-permute-start.44 = (bf16[192,384]{1,0:T(8,128)(2,1)S(1)}, bf16[192,384]{1,0:T(8,128)(2,1)S(1)}, u32[]{:S(2)}, u32[]{:S(2)}) collective-permute-start(bf16[192,384]{1,0:T(8,128)(2,1)S(1)} %get-tuple-element.130), channel_id=1, source_target_pairs={{0,24},{8,0},{16,8},{24,16},{1,25},{9,1},{17,9},{25,17},{2,26},{10... | collective-permute-start | bytes 442376 | tf_op jit(solution)/shard_map/ppermute | solution.py:607
  422.2 6.1 %collective-permute-start.61 = (bf16[3,192,384]{2,1,0:T(8,128)(2,1)S(1)}, bf16[3,192,384]{2,1,0:T(8,128)(2,1)S(1)}, u32[]{:S(2)}, u32[]{:S(2)}) collective-permute-start(bf16[3,192,384]{2,1,0:T(8,128)(2,1)S(1)} %pad_maximum_fusion.12), channel_id=1, source_target_pairs={{0,4},{4,0},{1,5},{5,1},{2,6},{6,2},{3,7},{7,3},{8,12},{12,8},{9,1... | collective-permute-start | bytes 1327112 | tf_op jit(solution)/shard_map/ppermute | solution.py:735
  (38 other events, 577.9 us)
